TPU v7x, 32 devices: a whole 2x2x4 slice. The times are simulated.
32 devices in a mesh: seq: 2 (over x), fsdp: 16 (over z, y, core).
Axes of the slice: x: 2, y: 2, z: 4, core: 2. Of those that a mesh axis runs over, the one named last changes fastest.
Arguments:
- inputs: bfloat16 [16, 1024, 1536], P('fsdp', 'seq'), may hold values from -6 to 6
- text_states: bfloat16 [16, 64, 1536], P('fsdp'), may hold values from -6 to 6
- adapter_index: int32 [16], P('fsdp'), may hold values from 0 to 7
- norm_gains: float32 [3, 1536], replicated, may hold values from 0.25 to 1.75
- norm_biases: float32 [3, 1536], replicated, may hold values from -1.8 to 1.8
- self_in: bfloat16 [1536, 4608], P('fsdp'), may hold values from -0.15625 to 0.15625
- self_out: bfloat16 [1536, 1536], P('fsdp'), may hold values from -2.5 to 2.5
- cross_query: bfloat16 [1536, 1536], P('fsdp'), may hold values from -0.15625 to 0.15625
- cross_text: bfloat16 [1536, 3072], P('fsdp'), may hold values from -0.15625 to 0.15625
- cross_out: bfloat16 [1536, 1536], P('fsdp'), may hold values from -0.875 to 0.875
- hidden_in: bfloat16 [1536, 6144], P('fsdp'), may hold values from -0.15625 to 0.15625
- hidden_out: bfloat16 [6144, 1536], P('fsdp'), may hold values from -0.078125 to 0.078125
- adapter_down: bfloat16 [8, 16, 19968], P(None, None, 'fsdp'), may hold values from -0.15625 to 0.15625
- adapter_up: bfloat16 [8, 16, 19968], P(None, None, 'fsdp'), may hold values from -0.75 to 0.75
- cotangent: bfloat16 [16, 1024, 1536], P('fsdp', 'seq'), may hold values from -6 to 6
Outputs:
- output: bfloat16 [16, 1024, 1536], P('fsdp', 'seq')
- grad_input: float32 [16, 1024, 1536], P('fsdp', 'seq')
- grad_text: float32 [16, 64, 1536], P('fsdp')
- grad_down: float32 [8, 16, 19968], P(None, None, 'fsdp')
- grad_up: float32 [8, 16, 19968], P(None, None, 'fsdp')
All inputs are finite; a program needn't handle non-finite values.
Results may differ from a plain program's by a relative error of at most 0.022.
Values may be sent and summed in bfloat16 or wider, within the bound.
No kernel may reach another device: no remote copies, remote signals or barrier semaphores. Data moves between devices by JAX's collectives and lax.ppermute only.
A program may use at most 448 MiB of HBM per device.

v0:
```python
from functools import partial

import jax
import jax.numpy as jnp
from jax import lax
from jax.sharding import PartitionSpec as P

D = 1536
HEAD = 64
FF = 6144
ADAPTERS = 8


def layer_norm(values, gains, biases):
    centered = values - jnp.mean(values, -1, keepdims=True)
    variance = jnp.mean(centered * centered, -1, keepdims=True)
    return centered * lax.rsqrt(variance + 1e-05) * gains + biases


def norm_back(values, gains, biases, gradient):
    _, pull_back = jax.vjp(lambda moving: layer_norm(moving, gains, biases), values)
    return pull_back(gradient)[0]


def adapter_slices(down_rows, upper_rows, index):
    in_cuts = [0, 3 * D, 4 * D, 5 * D, 7 * D, 8 * D, 9 * D, 9 * D + FF]
    out_cuts = [0, 3 * D, 4 * D, 5 * D, 7 * D, 8 * D, 8 * D + FF, 9 * D + FF]
    return (
        down_rows[..., in_cuts[index] : in_cuts[index + 1]],
        upper_rows[..., out_cuts[index] : out_cuts[index + 1]],
    )


def project(inputs, weight, pieces, part_count):
    down_rows, upper_rows = pieces
    clip_count, row_count, in_width = inputs.shape
    rank_size = down_rows.shape[1]
    down_split = down_rows.reshape(clip_count, rank_size, part_count, in_width)
    upper_split = upper_rows.reshape(clip_count, rank_size, part_count, -1)
    latent = jnp.einsum(
        "cti,crpi->ctpr", inputs, down_split, preferred_element_type=jnp.float32
    ).astype(jnp.bfloat16)
    adapted = jnp.einsum("ctpr,crpo->ctpo", latent, upper_split, preferred_element_type=jnp.float32)
    direct = jnp.einsum("cti,io->cto", inputs, weight, preferred_element_type=jnp.float32)
    return (direct + adapted.reshape(clip_count, row_count, -1), latent)


def project_back(inputs, latent, grad_low, weight, pieces, part_count):
    down_rows, upper_rows = pieces
    clip_count, row_count, in_width = inputs.shape
    rank_size = down_rows.shape[1]
    down_split = down_rows.reshape(clip_count, rank_size, part_count, in_width)
    upper_split = upper_rows.reshape(clip_count, rank_size, part_count, -1)
    grad_split = grad_low.reshape(clip_count, row_count, part_count, -1)
    upper_grad = jnp.einsum(
        "ctpr,ctpo->crpo", latent, grad_split, preferred_element_type=jnp.float32
    )
    latent_grad = jnp.einsum(
        "ctpo,crpo->ctpr", grad_split, upper_split, preferred_element_type=jnp.float32
    ).astype(jnp.bfloat16)
    down_grad = jnp.einsum(
        "ctpr,cti->crpi", latent_grad, inputs, preferred_element_type=jnp.float32
    )
    input_grad = jnp.einsum("cto,io->cti", grad_low, weight, preferred_element_type=jnp.float32)
    input_grad = input_grad + jnp.einsum(
        "ctpr,crpi->cti", latent_grad, down_split, preferred_element_type=jnp.float32
    )
    return (
        input_grad,
        down_grad.reshape(clip_count, rank_size, -1),
        upper_grad.reshape(clip_count, rank_size, -1),
    )


def masked_scores(query_block, key_split, row_start, block_rows, key_count, score_scale):
    scores = (
        jnp.einsum("cqhe,ckhe->chqk", query_block, key_split, preferred_element_type=jnp.float32)
        * score_scale
    )
    row_pos = row_start + lax.broadcasted_iota(jnp.int32, (block_rows, key_count), 0)
    col_pos = lax.broadcasted_iota(jnp.int32, (block_rows, key_count), 1)
    return jnp.where(col_pos <= row_pos, scores, -1e30)


def self_attention(queries, key_rows, values, score_scale):
    clip_count, frame_count, local_width = queries.shape
    head_count = local_width // HEAD
    block_rows = min(512, frame_count)
    block_count = frame_count // block_rows
    key_split = key_rows.reshape(clip_count, frame_count, head_count, HEAD)
    value_split = values.reshape(clip_count, frame_count, head_count, HEAD)
    outputs = []
    lse_blocks = []
    for block_index in range(block_count):
        row_start = block_index * block_rows
        key_count = row_start + block_rows
        query_block = queries[:, row_start:key_count].reshape(
            clip_count, block_rows, head_count, HEAD
        )
        scores = masked_scores(
            query_block, key_split[:, :key_count], row_start, block_rows, key_count, score_scale
        )
        row_top = jnp.max(scores, -1, keepdims=True)
        raised = jnp.exp(scores - row_top)
        row_total = jnp.sum(raised, -1, keepdims=True)
        prob_block = (raised / row_total).astype(jnp.bfloat16)
        mixed = jnp.einsum(
            "chqk,ckhe->cqhe",
            prob_block,
            value_split[:, :key_count],
            preferred_element_type=jnp.float32,
        )
        outputs.append(mixed.reshape(clip_count, block_rows, local_width).astype(jnp.bfloat16))
        lse_blocks.append((row_top + jnp.log(row_total))[..., 0])
    return (jnp.concatenate(outputs, 1), lse_blocks)


def self_attention_back(queries, key_rows, values, grad_out, lse_blocks, score_scale):
    clip_count, frame_count, local_width = queries.shape
    head_count = local_width // HEAD
    block_rows = min(512, frame_count)
    block_count = frame_count // block_rows
    key_split = key_rows.reshape(clip_count, frame_count, head_count, HEAD)
    value_split = values.reshape(clip_count, frame_count, head_count, HEAD)
    key_grad = jnp.zeros((clip_count, frame_count, head_count, HEAD), jnp.float32)
    value_grad = jnp.zeros((clip_count, frame_count, head_count, HEAD), jnp.float32)
    query_blocks = []
    for block_index in range(block_count):
        row_start = block_index * block_rows
        key_count = row_start + block_rows
        key_block = key_split[:, :key_count]
        value_block = value_split[:, :key_count]
        query_block = queries[:, row_start:key_count].reshape(
            clip_count, block_rows, head_count, HEAD
        )
        grad_block = grad_out[:, row_start:key_count].reshape(
            clip_count, block_rows, head_count, HEAD
        )
        scores = masked_scores(
            query_block, key_block, row_start, block_rows, key_count, score_scale
        )
        prob_block = jnp.exp(scores - lse_blocks[block_index][..., None])
        prob_grad = jnp.einsum(
            "cqhe,ckhe->chqk", grad_block, value_block, preferred_element_type=jnp.float32
        )
        score_grad = (
            prob_block * (prob_grad - jnp.sum(prob_block * prob_grad, -1, keepdims=True))
        ).astype(jnp.bfloat16)
        query_grad = (
            jnp.einsum("chqk,ckhe->cqhe", score_grad, key_block, preferred_element_type=jnp.float32)
            * score_scale
        )
        key_part = (
            jnp.einsum(
                "chqk,cqhe->ckhe", score_grad, query_block, preferred_element_type=jnp.float32
            )
            * score_scale
        )
        value_part = jnp.einsum(
            "chqk,cqhe->ckhe",
            prob_block.astype(jnp.bfloat16),
            grad_block,
            preferred_element_type=jnp.float32,
        )
        key_grad = key_grad.at[:, :key_count].add(key_part)
        value_grad = value_grad.at[:, :key_count].add(value_part)
        query_blocks.append(query_grad.reshape(clip_count, block_rows, local_width))
    query_grad = jnp.concatenate(query_blocks, 1)
    return (
        query_grad,
        key_grad.reshape(clip_count, frame_count, local_width),
        value_grad.reshape(clip_count, frame_count, local_width),
    )


def cross_forward(queries, key_rows, values, score_scale):
    clip_count, row_count, model_width = queries.shape
    head_count = model_width // HEAD
    query_split = queries.reshape(clip_count, row_count, head_count, HEAD)
    key_split = key_rows.reshape(clip_count, key_rows.shape[1], head_count, HEAD)
    value_split = values.reshape(clip_count, values.shape[1], head_count, HEAD)
    scores = (
        jnp.einsum("cqhe,ckhe->chqk", query_split, key_split, preferred_element_type=jnp.float32)
        * score_scale
    )
    raised = jnp.exp(scores - jnp.max(scores, -1, keepdims=True))
    prob_all = raised / jnp.sum(raised, -1, keepdims=True)
    mixed = jnp.einsum(
        "chqk,ckhe->cqhe",
        prob_all.astype(jnp.bfloat16),
        value_split,
        preferred_element_type=jnp.float32,
    )
    return (mixed.reshape(clip_count, row_count, model_width).astype(jnp.bfloat16), prob_all)


def cross_backward(queries, key_rows, values, prob_all, grad_low, score_scale):
    clip_count, row_count, model_width = queries.shape
    head_count = model_width // HEAD
    text_count = key_rows.shape[1]
    query_split = queries.reshape(clip_count, row_count, head_count, HEAD)
    key_split = key_rows.reshape(clip_count, text_count, head_count, HEAD)
    value_split = values.reshape(clip_count, text_count, head_count, HEAD)
    grad_split = grad_low.reshape(clip_count, row_count, head_count, HEAD)
    prob_grad = jnp.einsum(
        "cqhe,ckhe->chqk", grad_split, value_split, preferred_element_type=jnp.float32
    )
    score_grad = (prob_all * (prob_grad - jnp.sum(prob_all * prob_grad, -1, keepdims=True))).astype(
        jnp.bfloat16
    )
    query_grad = (
        jnp.einsum("chqk,ckhe->cqhe", score_grad, key_split, preferred_element_type=jnp.float32)
        * score_scale
    )
    key_grad = (
        jnp.einsum("chqk,cqhe->ckhe", score_grad, query_split, preferred_element_type=jnp.float32)
        * score_scale
    )
    value_grad = jnp.einsum(
        "chqk,cqhe->ckhe",
        prob_all.astype(jnp.bfloat16),
        grad_split,
        preferred_element_type=jnp.float32,
    )
    memory_grad = jnp.concatenate(
        [
            key_grad.reshape(clip_count, text_count, model_width),
            value_grad.reshape(clip_count, text_count, model_width),
        ],
        -1,
    )
    return (
        query_grad.reshape(clip_count, row_count, model_width).astype(jnp.bfloat16),
        memory_grad.astype(jnp.bfloat16),
    )


def body(
    inputs,
    text_states,
    adapter_index,
    norm_gains,
    norm_biases,
    self_in,
    self_out,
    cross_query,
    cross_text,
    cross_out,
    hidden_in,
    hidden_out,
    adapter_down,
    adapter_up,
    cotangent,
):
    score_scale = float(HEAD) ** (-0.5)
    tables = (
        lax.all_gather(adapter_down, "fsdp", axis=2, tiled=True),
        lax.all_gather(adapter_up, "fsdp", axis=2, tiled=True),
    )
    selector = adapter_index[:, None] == jnp.arange(ADAPTERS, dtype=jnp.int32)[None, :]
    picker = selector.astype(jnp.bfloat16)
    down_pick = jnp.einsum(
        "ca,arw->crw", picker, tables[0], preferred_element_type=jnp.float32
    ).astype(jnp.bfloat16)
    upper_pick = jnp.einsum(
        "ca,arw->crw", picker, tables[1], preferred_element_type=jnp.float32
    ).astype(jnp.bfloat16)
    slices = [adapter_slices(down_pick, upper_pick, index) for index in range(7)]
    self_weights = (
        lax.all_gather(self_in, "fsdp", axis=0, tiled=True),
        lax.all_gather(self_out, "fsdp", axis=0, tiled=True),
    )
    resid0 = inputs.astype(jnp.float32)
    normed1 = layer_norm(resid0, norm_gains[0], norm_biases[0]).astype(jnp.bfloat16)
    triple, latent_qkv = project(normed1, self_weights[0], slices[0], 3)
    triple = triple.astype(jnp.bfloat16)
    head_q, head_k, head_v = (
        lax.all_to_all(triple[..., :D], "seq", split_axis=2, concat_axis=1, tiled=True),
        lax.all_to_all(triple[..., D : 2 * D], "seq", split_axis=2, concat_axis=1, tiled=True),
        lax.all_to_all(triple[..., 2 * D :], "seq", split_axis=2, concat_axis=1, tiled=True),
    )
    head_out, lse_blocks = self_attention(head_q, head_k, head_v, score_scale)
    attended = lax.all_to_all(head_out, "seq", split_axis=1, concat_axis=2, tiled=True)
    branch_one, latent_so = project(attended, self_weights[1], slices[1], 1)
    resid1 = resid0 + branch_one
    cross_weights = (
        lax.all_gather(cross_query, "fsdp", axis=0, tiled=True),
        lax.all_gather(cross_text, "fsdp", axis=0, tiled=True),
        lax.all_gather(cross_out, "fsdp", axis=0, tiled=True),
    )
    normed2 = layer_norm(resid1, norm_gains[1], norm_biases[1]).astype(jnp.bfloat16)
    cross_queries, latent_cq = project(normed2, cross_weights[0], slices[2], 1)
    cross_queries = cross_queries.astype(jnp.bfloat16)
    memory, latent_ct = project(text_states, cross_weights[1], slices[3], 2)
    memory = memory.astype(jnp.bfloat16)
    cross_keys = memory[..., :D]
    cross_values = memory[..., D:]
    cross_attended, cross_probs = cross_forward(
        cross_queries, cross_keys, cross_values, score_scale
    )
    branch_two, latent_co = project(cross_attended, cross_weights[2], slices[4], 1)
    resid2 = resid1 + branch_two
    hidden_weights = (
        lax.all_gather(hidden_in, "fsdp", axis=0, tiled=True),
        lax.all_gather(hidden_out, "fsdp", axis=0, tiled=True),
    )
    normed3 = layer_norm(resid2, norm_gains[2], norm_biases[2]).astype(jnp.bfloat16)
    pre_act, latent_h1 = project(normed3, hidden_weights[0], slices[5], 1)
    activated = jax.nn.gelu(pre_act, approximate=False).astype(jnp.bfloat16)
    branch_three, latent_h2 = project(activated, hidden_weights[1], slices[6], 1)
    output = (resid2 + branch_three).astype(jnp.bfloat16)
    top_grad = cotangent.astype(jnp.float32)
    act_grad, down_h2, upper_h2 = project_back(
        activated, latent_h2, cotangent, hidden_weights[1], slices[6], 1
    )
    _, gelu_pull = jax.vjp(partial(jax.nn.gelu, approximate=False), pre_act)
    pre_grad = gelu_pull(act_grad)[0].astype(jnp.bfloat16)
    normed3_grad, down_h1, upper_h1 = project_back(
        normed3, latent_h1, pre_grad, hidden_weights[0], slices[5], 1
    )
    resid2_grad = top_grad + norm_back(resid2, norm_gains[2], norm_biases[2], normed3_grad)
    cross_grad, down_co, upper_co = project_back(
        cross_attended, latent_co, resid2_grad.astype(jnp.bfloat16), cross_weights[2], slices[4], 1
    )
    cq_grad, memory_grad = cross_backward(
        cross_queries,
        cross_keys,
        cross_values,
        cross_probs,
        cross_grad.astype(jnp.bfloat16),
        score_scale,
    )
    normed2_grad, down_cq, upper_cq = project_back(
        normed2, latent_cq, cq_grad, cross_weights[0], slices[2], 1
    )
    text_grad, down_ct, upper_ct = project_back(
        text_states, latent_ct, memory_grad, cross_weights[1], slices[3], 2
    )
    resid1_grad = resid2_grad + norm_back(resid1, norm_gains[1], norm_biases[1], normed2_grad)
    attended_grad, down_so, upper_so = project_back(
        attended, latent_so, resid1_grad.astype(jnp.bfloat16), self_weights[1], slices[1], 1
    )
    head_grad = lax.all_to_all(
        attended_grad.astype(jnp.bfloat16), "seq", split_axis=2, concat_axis=1, tiled=True
    )
    hq_grad, hk_grad, hv_grad = self_attention_back(
        head_q, head_k, head_v, head_grad, lse_blocks, score_scale
    )
    frame_q, frame_k, frame_v = (
        lax.all_to_all(
            hq_grad.astype(jnp.bfloat16), "seq", split_axis=1, concat_axis=2, tiled=True
        ),
        lax.all_to_all(
            hk_grad.astype(jnp.bfloat16), "seq", split_axis=1, concat_axis=2, tiled=True
        ),
        lax.all_to_all(
            hv_grad.astype(jnp.bfloat16), "seq", split_axis=1, concat_axis=2, tiled=True
        ),
    )
    triple_grad = jnp.concatenate([frame_q, frame_k, frame_v], -1)
    normed1_grad, down_qkv, upper_qkv = project_back(
        normed1, latent_qkv, triple_grad, self_weights[0], slices[0], 3
    )
    input_grad = resid1_grad + norm_back(resid0, norm_gains[0], norm_biases[0], normed1_grad)
    down_all = jnp.concatenate([down_qkv, down_so, down_cq, down_ct, down_co, down_h1, down_h2], -1)
    upper_all = jnp.concatenate(
        [upper_qkv, upper_so, upper_cq, upper_ct, upper_co, upper_h1, upper_h2], -1
    )
    selector_float = selector.astype(jnp.float32)
    table_down = jnp.einsum(
        "ca,crw->arw", selector_float, down_all, precision=lax.Precision.HIGHEST
    )
    table_up = jnp.einsum("ca,crw->arw", selector_float, upper_all, precision=lax.Precision.HIGHEST)
    shares = (
        lax.psum_scatter(
            table_down.astype(jnp.bfloat16), "fsdp", scatter_dimension=2, tiled=True
        ).astype(jnp.float32),
        lax.psum_scatter(
            table_up.astype(jnp.bfloat16), "fsdp", scatter_dimension=2, tiled=True
        ).astype(jnp.float32),
    )
    text_total, down_total, upper_total = (
        lax.psum(text_grad.astype(jnp.bfloat16), "seq").astype(jnp.float32),
        lax.psum(shares[0].astype(jnp.bfloat16), "seq").astype(jnp.float32),
        lax.psum(shares[1].astype(jnp.bfloat16), "seq").astype(jnp.float32),
    )
    return (output, input_grad, text_total, down_total, upper_total)


def solution(mesh):
    return jax.shard_map(
        body,
        mesh=mesh,
        in_specs=(
            P("fsdp", "seq", None),
            P("fsdp", None, None),
            P("fsdp"),
            P(),
            P(),
            P("fsdp", None),
            P("fsdp", None),
            P("fsdp", None),
            P("fsdp", None),
            P("fsdp", None),
            P("fsdp", None),
            P("fsdp", None),
            P(None, None, "fsdp"),
            P(None, None, "fsdp"),
            P("fsdp", "seq", None),
        ),
        out_specs=(
            P("fsdp", "seq", None),
            P("fsdp", "seq", None),
            P("fsdp", None, None),
            P(None, None, "fsdp"),
            P(None, None, "fsdp"),
        ),
        check_vma=False,
    )
```

profile of v0, /device:TPU:0, one launch (start us, length us, event | category | flops | bytes accessed | tf_op | source)
XLA Modules:
  0.0 1659.9 jit_solution(7676458478315555427)
XLA Ops:
  21.8 194.5 %all-gather.14.cloned.1.call-done = bf16[8,16,19968]{1,0,2:T(8,128)(2,1)} async-done(((bf16[8,16,1248]{1,0,2:T(8,128)(2,1)}), bf16[8,16,19968]{1,0,2:T(8,128)(2,1)}) %all-gather.14.cloned.1.call-update) | async-done | bytes 5111824 | tf_op jit(solution)/shard_map/all_gather | solution.py:257
  216.3 39.2 %copy.311 = bf16[8,16,19968]{2,0,1:T(8,128)(2,1)} copy(bf16[8,16,19968]{1,0,2:T(8,128)(2,1)} %all-gather.14.cloned.1.call-done) | data formatting | bytes 10223616 | tf_op jit(solution)/shard_map/all_gather | solution.py:257
  260.6 160.0 %all-gather.12.cloned.1.call-done = bf16[8,16,19968]{1,0,2:T(8,128)(2,1)} async-done(((bf16[8,16,1248]{1,0,2:T(8,128)(2,1)}), bf16[8,16,19968]{1,0,2:T(8,128)(2,1)}) %all-gather.12.cloned.1.call-update) | async-done | bytes 5111824 | tf_op jit(solution)/shard_map/all_gather | solution.py:258
  420.6 38.8 %copy.309 = bf16[8,16,19968]{2,0,1:T(8,128)(2,1)} copy(bf16[8,16,19968]{1,0,2:T(8,128)(2,1)} %all-gather.12.cloned.1.call-done) | data formatting | bytes 10223616 | tf_op jit(solution)/shard_map/all_gather | solution.py:258
  480.9 52.7 %all-gather.10.cloned.1.call-done = bf16[1536,4608]{1,0:T(8,128)(2,1)} async-done(((bf16[96,4608]{1,0:T(8,128)(2,1)}), bf16[1536,4608]{1,0:T(8,128)(2,1)}) %all-gather.10.cloned.1.call-update) | async-done | bytes 14155792 | tf_op jit(solution)/shard_map/all_gather | solution.py:270
  533.6 14.1 fusion.16
  713.9 12.5 fusion.1
  768.5 17.0 %all-to-all-done.3 = bf16[2,2,196608]{2,1,0:T(2,128)(2,1)} async-done(((bf16[2,2,196608]{2,1,0:T(2,128)(2,1)}), bf16[2,2,196608]{2,1,0:T(2,128)(2,1)}, u32[]{:S(2)}, u32[]{:S(2)}) %all-to-all-start.3) | async-done | bytes 1572896 | tf_op jit(solution)/shard_map/all_to_all | solution.py:283
  838.7 37.8 %all-gather.24.cloned.1.call-done = bf16[1536,6144]{1,0:T(8,128)(2,1)} async-done(((bf16[96,6144]{1,0:T(8,128)(2,1)}), bf16[1536,6144]{1,0:T(8,128)(2,1)}) %all-gather.24.cloned.1.call-update) | async-done | bytes 18874384 | tf_op jit(solution)/shard_map/all_gather | solution.py:304
  876.5 41.5 %multiply_convert_fusion.2 = (bf16[512,6144]{1,0:T(8,128)(2,1)}, f32[512,6144]{1,0:T(8,128)}, f32[512,6144]{1,0:T(8,128)}) fusion(f32[6144,512]{0,1:T(8,128)} %fusion.146, bf16[512,1536]{1,0:T(8,128)(2,1)S(1)} %fusion.80, bf16[1536,6144]{1,0:T(8,128)(2,1)} %all-gather.24.cloned.1.call-done), kind=kOutput, calls=%fused_computation.18 | convolution fusion | flops 9871294464 | bytes 64487424 | tf_op jit(solution)/shard_map/cti,io->cto/dot_general | solution.py:44
  918.0 59.1 %all-gather.26.cloned.1.call-done = bf16[6144,1536]{1,0:T(8,128)(2,1)} async-done(((bf16[384,1536]{1,0:T(8,128)(2,1)}), bf16[6144,1536]{1,0:T(8,128)(2,1)}) %all-gather.26.cloned.1.call-update) | async-done | bytes 18874384 | tf_op jit(solution)/shard_map/all_gather | solution.py:305
  977.1 25.4 %add_convert_fusion = bf16[512,6144]{1,0:T(8,128)(2,1)} fusion(f32[512,6144]{1,0:T(8,128)} %get-tuple-element.83, f32[512,6144]{1,0:T(8,128)} %fusion.147, f32[512,6144]{1,0:T(8,128)} %get-tuple-element.105, bf16[6144,1536]{1,0:T(8,128)(2,1)} %all-gather.26.cloned.1.call-done, bf16[1,512,1536]{2,1,0:T(8,128)(2,1)S(1)} %copy-done.18), kind=kOutput, calls=%fused_computation.17 | convolution fusion | flops 9710862336 | bytes 64487424 | tf_op jit(solution)/shard_map/cto,io->cti/dot_general | solution.py:64
  1010.9 17.6 %fusion.55 = (f32[512]{0:T(512)S(1)}, f32[512,1536]{1,0:T(8,128)}) fusion(f32[1,512,1536]{2,1,0:T(8,128)S(1)} %copy-done.13, f32[512]{0:T(512)S(1)} %copy-done.119, f32[1536]{0:T(1024)S(1)} %copy-done.115, f32[512,1536]{1,0:T(8,128)} %fusion.160, bf16[512,6144]{1,0:T(8,128)(2,1)} %add_convert_fusion, bf16[1536,6144]{1,0:T(8,128)(2,1)} %all-gather.24.cloned.1.call-done), kind=kOutput, calls=%fused_computation.107 | convolution fusion | flops 9667608576 | bytes 34613248 | tf_op jit(solution)/shard_map/cto,io->cti/dot_general | solution.py:64
  1137.5 21.4 %multiply_reduce_fusion = (f32[12,512]{1,0:T(8,128)S(1)}, f32[12,512,1024]{2,1,0:T(8,128)}) fusion(f32[12,512]{1,0:T(8,128)S(1)} %copy-done.75, f32[12,512,1024]{2,1,0:T(8,128)} %get-tuple-element.96, pred[512,1024]{1,0:T(8,128)(4,1)S(1)} %copy-done.38, bf16[512,12,64]{0,2,1:T(8,128)(2,1)S(1)} %bitcast.741, bf16[1024,12,64]{0,2,1:T(8,128)(2,1)S(1)} %copy-done.50), kind=kOutput, calls=%fused_computation.2 | convolution fusion | flops 836757504 | bytes 53264384 | tf_op jit(solution)/shard_map/cqhe,ckhe->chqk/dot_general | solution.py:143
  1158.9 13.2 fusion.52
  1198.0 17.2 %multiply_convert_fusion = bf16[12,512,1024]{2,1,0:T(8,128)(2,1)S(1)} fusion(f32[12,512,1024]{2,1,0:T(8,128)} %get-tuple-element.115, f32[12,512]{1,0:T(8,128)S(1)} %get-tuple-element.114, f32[12,512]{1,0:T(8,128)S(1)} %copy-done.75, f32[12,512,1024]{2,1,0:T(8,128)} %get-tuple-element.96, pred[512,1024]{1,0:T(8,128)(4,1)} %iota_compare_fusion), kind=kLoop, calls=%fused_computation.1 | loop fusion | flops 37748736 | bytes 63488000 | tf_op jit(solution)/shard_map/convert_element_type | solution.py:148
  1368.1 32.9 %copy.324 = bf16[8,16,19968]{1,0,2:T(8,128)(2,1)} copy(bf16[8,16,19968]{2,1,0:T(8,128)(2,1)} %get-tuple-element.93) | data formatting | bytes 10223616
  1401.0 44.1 %reshape.1380 = bf16[19968,128]{1,0:T(8,128)(2,1)} reshape(bf16[19968,8,16]{2,1,0:T(8,128)(2,1)} %bitcast.679) | data formatting | bytes 10223616
  1446.9 33.0 %copy.322 = bf16[8,16,19968]{1,0,2:T(8,128)(2,1)} copy(bf16[8,16,19968]{2,1,0:T(8,128)(2,1)} %get-tuple-element.94) | data formatting | bytes 10223616
  1479.9 44.2 %reshape.1378 = bf16[19968,128]{1,0:T(8,128)(2,1)} reshape(bf16[19968,8,16]{2,1,0:T(8,128)(2,1)} %bitcast.680) | data formatting | bytes 10223616
  1533.9 17.5 %fusion.56 = bf16[1,512,1536]{2,1,0:T(8,128)(2,1)} fusion(f32[1,512,1536]{2,1,0:T(8,128)S(1)} %copy-done.14, f32[512,1536]{1,0:T(8,128)S(1)} %convolution_bitcast_fusion.3, bf16[512,6144]{1,0:T(8,128)(2,1)} %get-tuple-element.82, bf16[6144,1536]{1,0:T(8,128)(2,1)} %all-gather.26.cloned.1.call-done), kind=kOutput, calls=%fused_computation.119 | convolution fusion | flops 9666035712 | bytes 33030144 | tf_op jit(solution)/shard_map/cti,io->cto/dot_general | solution.py:44
  1560.4 15.3 fusion.51
  1585.8 19.0 %reduce-scatter.7.cloned.1.call-done = bf16[1248,128]{1,0:T(8,128)(2,1)} async-done(((bf16[19968,128]{1,0:T(8,128)(2,1)}), bf16[1248,128]{1,0:T(8,128)(2,1)}) %reduce-scatter.7.cloned.1.call-update) | async-done | bytes 319504
  1617.8 29.6 %all-reduce.5.cloned.1.call-done = (bf16[1,64,1536]{2,1,0:T(8,128)(2,1)}, bf16[8,16,1248]{2,1,0:T(8,128)(2,1)}, bf16[8,16,1248]{2,1,0:T(8,128)(2,1)}) async-done(((bf16[1,64,1536]{2,1,0:T(8,128)(2,1)}, bf16[8,16,1248]{2,1,0:T(8,128)(2,1)}, bf16[8,16,1248]{2,1,0:T(8,128)(2,1)}), (bf16[1,64,1536]{2,1,0:T(8,128)(2,1)}, bf16[8,16,1248]{2,1,0:T(8,128)(2,1)}, ...) | async-done | bytes 835600 | tf_op jit(solution)/shard_map/psum | solution.py:383
  (537 shorter events, 645.3 us)
Async XLA Ops:
  7.2 633.6 %copy-start = (bf16[1,64,1536]{2,1,0:T(8,128)(2,1)S(1)}, bf16[1,64,1536]{2,1,0:T(8,128)(2,1)}, u32[]{:S(2)}) copy-start(bf16[1,64,1536]{2,1,0:T(8,128)(2,1)} %param.28) | copy-start | bytes 589828
  7.2 209.1 %all-gather.14.cloned.1.call-start = ((), (), s32[]{:S(2)}) async-start(), calls=%async_computation.12 | async-start | bytes 43450368 | tf_op jit(solution)/shard_map/all_gather | solution.py:257
  10.8 409.8 %all-gather.12.cloned.1.call-start = ((), (), s32[]{:S(2)}) async-start(), calls=%async_computation.11 | async-start | bytes 43450368 | tf_op jit(solution)/shard_map/all_gather | solution.py:258
  13.6 520.0 %all-gather.10.cloned.1.call-start = ((), (), s32[]{:S(2)}) async-start(), calls=%async_computation.10 | async-start | bytes 15040512 | tf_op jit(solution)/shard_map/all_gather | solution.py:270
  14.3 628.7 %all-gather.18.cloned.1.call-start = ((), (), s32[]{:S(2)}) async-start(), calls=%async_computation.14 | async-start | bytes 10027008 | tf_op jit(solution)/shard_map/all_gather | solution.py:288
  14.9 777.4 %all-gather.16.cloned.1.call-start = ((), (), s32[]{:S(2)}) async-start(), calls=%async_computation.13 | async-start | bytes 5013504 | tf_op jit(solution)/shard_map/all_gather | solution.py:271
  15.5 787.4 %all-gather.20.cloned.1.call-start = ((), (), s32[]{:S(2)}) async-start(), calls=%async_computation.15 | async-start | bytes 5013504 | tf_op jit(solution)/shard_map/all_gather | solution.py:287
  16.1 806.4 %all-gather.22.cloned.1.call-start = ((), (), s32[]{:S(2)}) async-start(), calls=%async_computation.16 | async-start | bytes 5013504 | tf_op jit(solution)/shard_map/all_gather | solution.py:289
  16.8 859.7 %all-gather.24.cloned.1.call-start = ((), (), s32[]{:S(2)}) async-start(), calls=%async_computation.17 | async-start | bytes 20054016 | tf_op jit(solution)/shard_map/all_gather | solution.py:304
  17.6 959.5 %all-gather.26.cloned.1.call-start = ((), (), s32[]{:S(2)}) async-start(), calls=%async_computation.18 | async-start | bytes 20054016 | tf_op jit(solution)/shard_map/all_gather | solution.py:305
  21.8 511.8 %copy-start.24 = (bf16[1,512,1536]{2,1,0:T(8,128)(2,1)}, bf16[1,512,1536]{2,1,0:T(8,128)(2,1)S(1)}, u32[]{:S(2)}) copy-start(bf16[1,512,1536]{2,1,0:T(8,128)(2,1)S(1)} %fusion.50) | copy-start | bytes 4718596
  260.6 203.7 %copy-start.64 = (bf16[16,3,1536]{2,1,0:T(4,128)(2,1)}, bf16[16,3,1536]{2,1,0:T(4,128)(2,1)S(1)}, u32[]{:S(2)}) copy-start(bf16[16,3,1536]{2,1,0:T(4,128)(2,1)S(1)} %reshape.1290) | copy-start | bytes 442372
  571.6 29.7 %all-to-all-start.2 = ((bf16[2,2,196608]{2,1,0:T(2,128)(2,1)}), bf16[2,2,196608]{2,1,0:T(2,128)(2,1)}, u32[]{:S(2)}, u32[]{:S(2)}) async-start(bf16[2,2,196608]{2,1,0:T(2,128)(2,1)} %reshape.1392), calls=%async_computation.2 | async-start | bytes 3145728 | tf_op jit(solution)/shard_map/all_to_all | solution.py:279
  601.3 34.3 %all-to-all-start = ((bf16[2,2,196608]{2,1,0:T(2,128)(2,1)}), bf16[2,2,196608]{2,1,0:T(2,128)(2,1)}, u32[]{:S(2)}, u32[]{:S(2)}) async-start(bf16[2,2,196608]{2,1,0:T(2,128)(2,1)} %reshape.1388), calls=%async_computation | async-start | bytes 3145728 | tf_op jit(solution)/shard_map/all_to_all | solution.py:280
  635.7 34.0 %all-to-all-start.1 = ((bf16[2,2,196608]{2,1,0:T(2,128)(2,1)}), bf16[2,2,196608]{2,1,0:T(2,128)(2,1)}, u32[]{:S(2)}, u32[]{:S(2)}) async-start(bf16[2,2,196608]{2,1,0:T(2,128)(2,1)} %reshape.1390), calls=%async_computation.1 | async-start | bytes 3145728 | tf_op jit(solution)/shard_map/all_to_all | solution.py:278
  760.6 24.9 %all-to-all-start.3 = ((bf16[2,2,196608]{2,1,0:T(2,128)(2,1)}), bf16[2,2,196608]{2,1,0:T(2,128)(2,1)}, u32[]{:S(2)}, u32[]{:S(2)}) async-start(bf16[2,2,196608]{2,1,0:T(2,128)(2,1)} %reshape.1394), calls=%async_computation.3 | async-start | bytes 3145728 | tf_op jit(solution)/shard_map/all_to_all | solution.py:283
  838.7 138.4 %copy-start.18 = (bf16[1,512,1536]{2,1,0:T(8,128)(2,1)S(1)}, bf16[1,512,1536]{2,1,0:T(8,128)(2,1)}, u32[]{:S(2)}) copy-start(bf16[1,512,1536]{2,1,0:T(8,128)(2,1)} %param.41) | copy-start | bytes 4718596
  1084.7 24.7 %all-to-all-start.4 = ((bf16[2,2,196608]{2,1,0:T(2,128)(2,1)}), bf16[2,2,196608]{2,1,0:T(2,128)(2,1)}, u32[]{:S(2)}, u32[]{:S(2)}) async-start(bf16[2,2,196608]{2,1,0:T(2,128)(2,1)} %reshape.1396), calls=%async_computation.4 | async-start | bytes 3145728 | tf_op jit(solution)/shard_map/all_to_all | solution.py:343
  1193.3 68.1 %all-to-all-start.7 = ((bf16[2,2,196608]{2,1,0:T(2,128)(2,1)}), bf16[2,2,196608]{2,1,0:T(2,128)(2,1)}, u32[]{:S(2)}, u32[]{:S(2)}) async-start(bf16[2,2,196608]{2,1,0:T(2,128)(2,1)} %reshape.1398), calls=%async_computation.7 | async-start | bytes 3145728 | tf_op jit(solution)/shard_map/all_to_all | solution.py:356
  1261.4 38.7 %all-to-all-start.5 = ((bf16[2,2,196608]{2,1,0:T(2,128)(2,1)}), bf16[2,2,196608]{2,1,0:T(2,128)(2,1)}, u32[]{:S(2)}, u32[]{:S(2)}) async-start(bf16[2,2,196608]{2,1,0:T(2,128)(2,1)} %reshape.1402), calls=%async_computation.5 | async-start | bytes 3145728 | tf_op jit(solution)/shard_map/all_to_all | solution.py:350
  1300.1 33.7 %all-to-all-start.6 = ((bf16[2,2,196608]{2,1,0:T(2,128)(2,1)}), bf16[2,2,196608]{2,1,0:T(2,128)(2,1)}, u32[]{:S(2)}, u32[]{:S(2)}) async-start(bf16[2,2,196608]{2,1,0:T(2,128)(2,1)} %reshape.1400), calls=%async_computation.6 | async-start | bytes 3145728 | tf_op jit(solution)/shard_map/all_to_all | solution.py:353
  1304.7 273.8 %reduce-scatter.9.cloned.1.call-start = ((), (), s32[]{:S(2)}) async-start(), calls=%async_computation.20 | async-start | bytes 5431296
  1445.1 159.7 %reduce-scatter.7.cloned.1.call-start = ((), (), s32[]{:S(2)}) async-start(), calls=%async_computation.19 | async-start | bytes 5431296
  1524.2 123.2 %all-reduce.5.cloned.1.call-start = ((), (), s32[]{:S(2)}) async-start(), calls=%async_computation.21 | async-start | bytes 1703936 | tf_op jit(solution)/shard_map/psum | solution.py:383
  (135 other events, 773.0 us)
Sparse Core Ops, SparseCore 0:
  11.0 205.3 all-gather.13
  217.9 202.6 all-gather.11
  422.9 110.6 all-gather.9
  535.7 79.6 all-gather.17
  617.5 51.5 all-gather.15
  671.2 51.8 all-gather.19
  725.4 51.9 all-gather.21
  779.0 97.4 all-gather.23
  878.1 98.9 all-gather.25
  1445.2 78.3 reduce-scatter.8
  1528.0 76.7 reduce-scatter.6
  1612.5 34.8 all-reduce.4
where the time goes:
time: 1670 us; the launch traced here: 1660 us
  waiting for transfers between devices  585 us (35%)
  local copies, waits for them, and re-layouts  473 us (28%)
  matrix products  369 us (22%)
  other arithmetic  177 us (11%)
  starting transfers between devices  38.7 us (2%)
  between operations  17 us (1%)
    unnamed x318, local copies, waits for them, and re-layouts  260 us
    all_gather x1, waiting for transfers between devices, body(): lax.all_gather(adapter_down, 'fsdp', axis=2, tiled=True)  195 us
    all_gather x1, waiting for transfers between devices, body(): lax.all_gather(adapter_up, 'fsdp', axis=2, tiled=True)  160 us
    unnamed x13, other arithmetic  101 us
    dot_general x7, matrix products, project(): jnp.einsum('cti,io->cto', inputs, weight, preferred_element_type=jnp.floa...  94.5 us
    dot_general x7, matrix products, project_back(): jnp.einsum('cto,io->cti', grad_low, weight, preferred_element_type=jnp.fl...  78.1 us
    all_gather x1, waiting for transfers between devices, body(): lax.all_gather(hidden_out, 'fsdp', axis=0, tiled=True)  59.1 us
    all_gather x1, waiting for transfers between devices, body(): lax.all_gather(self_in, 'fsdp', axis=0, tiled=True)  52.7 us
  transfers between devices with their start and end apart: 20, of which 9 were waited for; matrix products, arithmetic and copies ran while one was open for 41% of the time, Pallas kernels for 0%

commit v1 on v0

v1 whole, which is shorter than its diff:
```python
from functools import partial

import jax
import jax.numpy as jnp
from jax import lax
from jax.experimental import pallas as pl
from jax.experimental.pallas import tpu as pltpu
from jax.sharding import PartitionSpec as P

HEAD = 64
LANES = 128
QB = 256
BF = jnp.bfloat16
F32 = jnp.float32
SCALE = float(HEAD) ** (-0.5)
SQRT_HALF = 0.7071067811865476
INV_SQRT_2PI = 0.3989422804014327
VMEM_LIMIT = 60 * 1024 * 1024


def mm(a, b):
    return lax.dot_general(a, b, (((1,), (0,)), ((), ())), preferred_element_type=F32)


def mm_nt(a, b):
    return lax.dot_general(a, b, (((1,), (1,)), ((), ())), preferred_element_type=F32)


def mm_tn(a, b):
    return lax.dot_general(a, b, (((0,), (0,)), ((), ())), preferred_element_type=F32)


def norm_stats(values):
    centered = values - jnp.mean(values, -1, keepdims=True)
    variance = jnp.mean(centered * centered, -1, keepdims=True)
    inverse = lax.rsqrt(variance + 1e-05)
    return centered * inverse, inverse


def layer_norm(values, gains, biases):
    unit, _ = norm_stats(values)
    return unit * gains + biases


def norm_back(values, gains, gradient):
    unit, inverse = norm_stats(values)
    scaled = gradient * gains
    mean_one = jnp.mean(scaled, -1, keepdims=True)
    mean_two = jnp.mean(scaled * unit, -1, keepdims=True)
    return inverse * (scaled - mean_one - unit * mean_two)


def whole(shape):
    return pl.BlockSpec(shape, lambda *_: (0,) * len(shape))


def params(count=1):
    return pltpu.CompilerParams(
        dimension_semantics=("arbitrary",) * count, vmem_limit_bytes=VMEM_LIMIT
    )


def cost(flops, moved, special=0):
    return pl.CostEstimate(flops=int(flops), bytes_accessed=int(moved), transcendentals=int(special))


def window(packed, start, width, rows=None, steps=1, step=0):
    block = width // steps
    rows = packed.shape[0] if rows is None else rows
    if start % block == 0 and block % LANES == 0:
        base = start // block
        return packed, pl.BlockSpec((rows, block), lambda *at: (0, base + (at[step] if steps > 1 else 0)))
    return packed[:, start : start + width], pl.BlockSpec(
        (rows, block), lambda *at: (0, at[step] if steps > 1 else 0)
    )


def qkv_kernel(x_ref, gain_ref, bias_ref, down_ref, up_ref, w_ref, normed_ref, lat_ref, out_ref):
    row_count = x_ref.shape[0]

    @pl.when(pl.program_id(0) == 0)
    def _():
        step = 128

        def some(at, carry):
            rows = pl.ds(pl.multiple_of(at * step, step), step)
            normed = layer_norm(x_ref[rows, :].astype(F32), gain_ref[...], bias_ref[...]).astype(BF)
            normed_ref[rows, :] = normed
            lat_ref[rows, :] = mm_nt(normed, down_ref[...]).astype(BF)
            return carry

        lax.fori_loop(0, row_count // step, some, 0)

    for at in range(0, row_count, 512):
        rows = pl.ds(at, min(512, row_count))
        out_ref[rows, :] = (
            mm(normed_ref[rows, :], w_ref[...]) + mm(lat_ref[rows, :], up_ref[...])
        ).astype(BF)


def qkv_project(x_all, gains, biases, down, up, packed, start, width):
    row_count, model = x_all.shape
    steps = 3 if (width // 3) % LANES == 0 else 1
    operand, spec = window(packed, start, width, steps=steps)
    block = width // steps
    if steps == 3:
        up_spec = pl.BlockSpec((None, up.shape[1], block), lambda at: (at, 0, 0))
    else:
        up = up.transpose(1, 0, 2).reshape(up.shape[1], width)
        up_spec = whole(up.shape)
    ranks = down.shape[0]
    return pl.pallas_call(
        qkv_kernel,
        grid=(steps,),
        in_specs=[whole(x_all.shape), whole(gains.shape), whole(biases.shape), whole(down.shape), up_spec, spec],
        out_specs=[
            whole(x_all.shape),
            whole((row_count, ranks)),
            pl.BlockSpec((row_count, block), lambda at: (0, at)),
        ],
        out_shape=[
            jax.ShapeDtypeStruct(x_all.shape, BF),
            jax.ShapeDtypeStruct((row_count, ranks), BF),
            jax.ShapeDtypeStruct((row_count, width), BF),
        ],
        compiler_params=params(),
        cost_estimate=cost(2 * row_count * model * width, 2 * (row_count + width) * model),
        name="qkv_project",
    )(x_all, gains, biases, down, up, operand)


def tri_start(at):
    return QB * at * (at + 1) // 2


def attend_kernel(q_ref, k_ref, v_ref, out_ref, prob_ref, val_t_ref, out_t_ref):
    frames = q_ref.shape[0]
    lane = lax.broadcasted_iota(jnp.int32, (1, LANES), 1) // HEAD
    val_t_ref[...] = v_ref[...].T
    for half in range(2):
        keep = lane == half
        for at in range(frames // QB):
            stop = (at + 1) * QB
            query = q_ref[at * QB : stop, :] * jnp.where(keep, SCALE, 0.0).astype(BF)
            score = mm_nt(k_ref[0:stop, :], query)
            row = lax.broadcasted_iota(jnp.int32, (stop, QB), 0)
            col = lax.broadcasted_iota(jnp.int32, (stop, QB), 1) + at * QB
            score = jnp.where(row <= col, score, -1e30)
            raised = jnp.exp(score - jnp.max(score, 0, keepdims=True))
            prob = (raised * (1.0 / jnp.sum(raised, 0, keepdims=True))).astype(BF)
            prob_ref[half, tri_start(at) : tri_start(at) + stop, :] = prob
            mixed = mm(val_t_ref[half * HEAD : (half + 1) * HEAD, 0:stop], prob)
            out_t_ref[half * HEAD : (half + 1) * HEAD, at * QB : stop] = mixed
    out_ref[...] = out_t_ref[...].T.astype(BF)


def pair_specs(frames, width):
    pairs = width // LANES
    return [pl.BlockSpec((frames, LANES), lambda at, part=part: (0, part * pairs + at)) for part in range(3)]


def attend(triple, width):
    frames = triple.shape[0]
    pairs = width // LANES
    tri = tri_start(frames // QB)
    return pl.pallas_call(
        attend_kernel,
        grid=(pairs,),
        in_specs=pair_specs(frames, width),
        out_specs=[
            pl.BlockSpec((frames, LANES), lambda at: (0, at)),
            pl.BlockSpec((2, tri, QB), lambda at: (at, 0, 0)),
        ],
        out_shape=[
            jax.ShapeDtypeStruct((frames, width), BF),
            jax.ShapeDtypeStruct((2 * pairs, tri, QB), BF),
        ],
        scratch_shapes=[pltpu.VMEM((LANES, frames), BF), pltpu.VMEM((LANES, frames), F32)],
        compiler_params=params(),
        cost_estimate=cost(
            8 * tri * QB * HEAD * pairs, 2 * (4 * frames * width + 2 * pairs * tri * QB), 2 * pairs * tri * QB
        ),
        name="attend",
    )(triple, triple, triple)


def attend_back_kernel(
    q_ref, k_ref, v_ref, out_ref, grad_ref, prob_ref, back_ref, key_t_ref, dq_t_ref, dk_acc, dv_acc
):
    frames = q_ref.shape[0]
    lane = lax.broadcasted_iota(jnp.int32, (1, LANES), 1) // HEAD
    key_t_ref[...] = k_ref[...].T
    dk_acc[...] = jnp.zeros_like(dk_acc)
    dv_acc[...] = jnp.zeros_like(dv_acc)
    for at in range(frames // QB):
        stop = (at + 1) * QB
        rows = slice(at * QB, stop)
        product = (out_ref[rows, :].astype(F32) * grad_ref[rows, :].astype(F32)).T
        for half in range(2):
            keep = lane == half
            mask = jnp.where(keep, 1.0, 0.0).astype(BF)
            query = q_ref[rows, :] * jnp.where(keep, SCALE, 0.0).astype(BF)
            grad = grad_ref[rows, :] * mask
            delta = jnp.sum(product[half * HEAD : (half + 1) * HEAD, :], 0, keepdims=True)
            prob = prob_ref[half, tri_start(at) : tri_start(at) + stop, :]
            prob_grad = mm_nt(v_ref[0:stop, :], grad)
            score_grad = (prob.astype(F32) * (prob_grad - delta)).astype(BF)
            dv_acc[0:stop, :] += mm(prob, grad)
            dk_acc[0:stop, :] += mm(score_grad, query)
            dq_t_ref[half * HEAD : (half + 1) * HEAD, rows] = mm(
                key_t_ref[half * HEAD : (half + 1) * HEAD, 0:stop], score_grad
            )
    back_ref[0] = (dq_t_ref[...].T * SCALE).astype(BF)
    back_ref[1] = dk_acc[...].astype(BF)
    back_ref[2] = dv_acc[...].astype(BF)


def attend_back(triple, attended, gradient, probs, width):
    frames = triple.shape[0]
    pairs = width // LANES
    tri = tri_start(frames // QB)
    column = pl.BlockSpec((frames, LANES), lambda at: (0, at))
    return pl.pallas_call(
        attend_back_kernel,
        grid=(pairs,),
        in_specs=pair_specs(frames, width) + [column, column, pl.BlockSpec((2, tri, QB), lambda at: (at, 0, 0))],
        out_specs=pl.BlockSpec((3, frames, LANES), lambda at: (0, 0, at)),
        out_shape=jax.ShapeDtypeStruct((3, frames, width), BF),
        scratch_shapes=[
            pltpu.VMEM((LANES, frames), BF),
            pltpu.VMEM((LANES, frames), F32),
            pltpu.VMEM((frames, LANES), F32),
            pltpu.VMEM((frames, LANES), F32),
        ],
        compiler_params=params(),
        cost_estimate=cost(16 * tri * QB * HEAD * pairs, 2 * (8 * frames * width + 2 * pairs * tri * QB)),
        name="attend_back",
    )(triple, triple, triple, attended, gradient, probs)


def feed_kernel(
    normed_ref, cot_ref, down_in_ref, up_in_ref, down_out_ref, up_out_ref, w_in_ref, w_out_ref,
    out_ref, gu_ref, gdown_in_ref, gup_in_ref, gdown_out_ref, gup_out_ref,
    out_acc, gu_acc, lat_in, glat_out, lat_acc, glat_acc, lat_t, glat_t,
):
    at = pl.program_id(0)

    @pl.when(at == 0)
    def _():
        latent = mm_nt(normed_ref[...], down_in_ref[...]).astype(BF)
        glat = mm_nt(cot_ref[...], up_out_ref[...]).astype(BF)
        lat_in[...] = latent
        glat_out[...] = glat
        lat_t[...] = latent.astype(F32).T.astype(BF)
        glat_t[...] = glat.astype(F32).T.astype(BF)
        out_acc[...] = jnp.zeros_like(out_acc)
        gu_acc[...] = jnp.zeros_like(gu_acc)
        lat_acc[...] = jnp.zeros_like(lat_acc)
        glat_acc[...] = jnp.zeros_like(glat_acc)

    w_in = w_in_ref[...]
    w_out = w_out_ref[...]
    pre = mm(normed_ref[...], w_in) + mm(lat_in[...], up_in_ref[...])
    act_grad = mm_nt(cot_ref[...], w_out) + mm(glat_out[...], down_out_ref[...])
    cdf = 0.5 * (1.0 + lax.erf(pre * SQRT_HALF))
    slope = cdf + pre * (jnp.exp(-0.5 * pre * pre) * INV_SQRT_2PI)
    act = (pre * cdf).astype(BF)
    pre_grad = (act_grad * slope).astype(BF)
    out_acc[...] += mm(act, w_out)
    gu_acc[...] += mm_nt(pre_grad, w_in)
    lat_acc[...] += mm_nt(act, down_out_ref[...])
    glat_acc[...] += mm_nt(pre_grad, up_in_ref[...])
    gup_in_ref[...] = mm(lat_t[...], pre_grad)
    gdown_out_ref[...] = mm(glat_t[...], act)

    @pl.when(at == pl.num_programs(0) - 1)
    def _():
        latent = lat_acc[...].astype(BF)
        glat = glat_acc[...].astype(BF)
        out_ref[...] = (out_acc[...] + mm(latent, up_out_ref[...])).astype(out_ref.dtype)
        gu_ref[...] = (gu_acc[...] + mm(glat, down_in_ref[...])).astype(gu_ref.dtype)
        gup_out_ref[...] = mm(latent.astype(F32).T.astype(BF), cot_ref[...])
        gdown_in_ref[...] = mm(glat.astype(F32).T.astype(BF), normed_ref[...])


def feed_forward(normed, cotangent, down_in, up_in, down_out, up_out, weights, hidden, kind):
    row_count, model = normed.shape
    rank = down_in.shape[0]
    block = 512 if hidden % 512 == 0 else (256 if hidden % 256 == 0 else hidden)
    w_in, in_spec, w_out, out_spec = weights(block)
    main = whole((row_count, model))
    slim = pl.BlockSpec((rank, block), lambda at: (0, at))
    small = whole((rank, model))
    return pl.pallas_call(
        feed_kernel,
        grid=(hidden // block,),
        in_specs=[main, main, small, slim, slim, small, in_spec, out_spec],
        out_specs=[main, main, small, slim, slim, small],
        out_shape=[
            jax.ShapeDtypeStruct((row_count, model), kind),
            jax.ShapeDtypeStruct((row_count, model), kind),
            jax.ShapeDtypeStruct((rank, model), F32),
            jax.ShapeDtypeStruct((rank, hidden), F32),
            jax.ShapeDtypeStruct((rank, hidden), F32),
            jax.ShapeDtypeStruct((rank, model), F32),
        ],
        scratch_shapes=[pltpu.VMEM((row_count, model), F32)] * 2
        + [pltpu.VMEM((row_count, rank), BF)] * 2
        + [pltpu.VMEM((row_count, rank), F32)] * 2
        + [pltpu.VMEM((rank, row_count), BF)] * 2,
        compiler_params=params(),
        cost_estimate=cost(8 * row_count * model * hidden, 4 * hidden * model, 2 * row_count * hidden),
        name="feed_forward",
    )(normed, cotangent, down_in, up_in, down_out, up_out, w_in, w_out)


def spread_heads(rows_ref, into_ref, model):
    keys = rows_ref.shape[0]
    wide = 4 * HEAD
    row = lax.broadcasted_iota(jnp.int32, (4 * keys, wide), 0) // keys
    col = lax.broadcasted_iota(jnp.int32, (4 * keys, wide), 1) // HEAD
    mask = jnp.where(row == col, 1.0, 0.0).astype(BF)
    for group in range(model // wide):
        part = rows_ref[:, group * wide : (group + 1) * wide]
        into_ref[group * 4 * keys : (group + 1) * 4 * keys, :] = jnp.concatenate([part] * 4, 0) * mask


def half_sums(values, reduce, fill):
    pieces = []
    for at in range(values.shape[1] // LANES):
        piece = values[:, at * LANES : (at + 1) * LANES]
        low = lax.broadcasted_iota(jnp.int32, piece.shape, 1) < HEAD
        first = reduce(jnp.where(low, piece, fill), -1, keepdims=True)
        second = reduce(jnp.where(low, fill, piece), -1, keepdims=True)
        pieces.append(jnp.where(low, first, second))
    return jnp.concatenate(pieces, 1)


def middle_kernel(
    attended_ref, inputs_ref, w_self_ref, w_query_ref, w_cross_ref, adapt_ref, gain_ref, bias_ref, keys_ref, values_ref,
    resid1_ref, normed2_ref, query_ref, probs_ref, crossed_ref, resid2_ref, normed3_ref, lat_ref,
    key_wide, value_wide,
):
    model = attended_ref.shape[1]
    wide = 4 * HEAD

    @pl.when(pl.program_id(0) == 0)
    def _():
        spread_heads(keys_ref, key_wide, model)
        spread_heads(values_ref, value_wide, model)

    def adapted(moving, weight, index):
        latent = mm_nt(moving, adapt_ref[32 * index : 32 * index + 16, :]).astype(BF)
        lat_ref[:, 16 * index : 16 * index + 16] = latent
        return mm(moving, weight[...]) + mm(latent, adapt_ref[32 * index + 16 : 32 * index + 32, :])

    resid1 = inputs_ref[...].astype(F32) + adapted(attended_ref[...], w_self_ref, 0)
    resid1_ref[...] = resid1
    normed2 = layer_norm(resid1, gain_ref[1:2, :], bias_ref[1:2, :]).astype(BF)
    normed2_ref[...] = normed2
    query = adapted(normed2, w_query_ref, 1).astype(BF)
    query_ref[...] = query
    for group in range(model // wide):
        lanes = slice(group * wide, (group + 1) * wide)
        score = mm_nt(query[:, lanes], key_wide[lanes, :]) * SCALE
        raised = jnp.exp(score - half_sums(score, jnp.max, -1e30))
        prob = (raised / half_sums(raised, jnp.sum, 0.0)).astype(BF)
        probs_ref[:, lanes] = prob
        crossed_ref[:, lanes] = mm(prob, value_wide[lanes, :]).astype(BF)
    resid2 = resid1 + adapted(crossed_ref[...], w_cross_ref, 2)
    resid2_ref[...] = resid2
    normed3_ref[...] = layer_norm(resid2, gain_ref[2:3, :], bias_ref[2:3, :]).astype(BF)


def once(shape, at=None):
    spot = (0,) * len(shape) if at is None else at
    return pl.BlockSpec(shape, lambda *_: spot, pipeline_mode=pl.Buffered(1))


def square(packed, start):
    model = packed.shape[0]
    return packed, once((model, model), (0, start // model))


def middle(attended, inputs, packed, starts, adapters, gains, biases, keys, values):
    row_count, model = attended.shape
    step = min(row_count, 256)
    (w_self, spec_self), (w_query, spec_query), (w_cross, spec_cross) = [square(packed, at) for at in starts]
    rows = pl.BlockSpec((step, model), lambda at: (at, 0))
    shape = lambda kind: jax.ShapeDtypeStruct((row_count, model), kind)
    return pl.pallas_call(
        middle_kernel,
        grid=(row_count // step,),
        in_specs=[rows, rows, spec_self, spec_query, spec_cross]
        + [once(item.shape) for item in (adapters, gains, biases, keys, values)],
        out_specs=[rows] * 7 + [pl.BlockSpec((step, 48), lambda at: (at, 0))],
        out_shape=[shape(kind) for kind in (F32, BF, BF, BF, BF, F32, BF)]
        + [jax.ShapeDtypeStruct((row_count, 48), BF)],
        scratch_shapes=[pltpu.VMEM((model // HEAD * keys.shape[0], 4 * HEAD), BF)] * 2,
        compiler_params=params(),
        cost_estimate=cost(6 * row_count * model * model, 6 * model * model + 24 * row_count * model),
        name="middle",
    )(attended, inputs, w_self, w_query, w_cross, adapters, gains, biases, keys, values)


def middle_back_kernel(
    gu_ref, more_ref, cot_ref, resid2_ref, resid1_ref, normed2_ref, query_ref, probs_ref, crossed_ref, attended_ref,
    lat_ref, w_self_ref, w_query_ref, w_cross_ref, adapt_ref, gain_ref, keys_ref, values_ref,
    resid1_grad_ref, attended_grad_ref, memory_ref, small_ref,
    key_wide, value_wide, key_acc, value_acc,
):
    model = gu_ref.shape[1]
    wide = 4 * HEAD
    keys = keys_ref.shape[0]
    at = pl.program_id(0)

    @pl.when(at == 0)
    def _():
        spread_heads(keys_ref, key_wide, model)
        spread_heads(values_ref, value_wide, model)
        key_acc[...] = jnp.zeros_like(key_acc)
        value_acc[...] = jnp.zeros_like(value_acc)
        small_ref[...] = jnp.zeros_like(small_ref)

    def back(gradient, moving, weight, index):
        down = adapt_ref[32 * index : 32 * index + 16, :]
        upper = adapt_ref[32 * index + 16 : 32 * index + 32, :]
        glat = mm_nt(gradient, upper).astype(BF)
        small_ref[32 * index : 32 * index + 16, :] += mm_tn(glat, moving)
        small_ref[32 * index + 16 : 32 * index + 32, :] += mm_tn(lat_ref[:, 16 * index : 16 * index + 16], gradient)
        return mm_nt(gradient, weight[...]) + mm(glat, down)

    gradient = gu_ref[...].astype(F32) + more_ref[...].astype(F32)
    resid2_grad = cot_ref[...].astype(F32) + norm_back(resid2_ref[...], gain_ref[2:3, :], gradient)
    cross_grad = back(resid2_grad.astype(BF), crossed_ref[...], w_cross_ref, 2).astype(BF)
    pieces = []
    for group in range(model // wide):
        lanes = slice(group * wide, (group + 1) * wide)
        part = cross_grad[:, lanes]
        prob = probs_ref[:, lanes]
        wide_prob = prob.astype(F32)
        weighted = wide_prob * mm_nt(part, value_wide[lanes, :])
        score_grad = (weighted - wide_prob * half_sums(weighted, jnp.sum, 0.0)).astype(BF)
        pieces.append((mm(score_grad, key_wide[lanes, :]) * SCALE).astype(BF))
        key_acc[lanes, :] += mm_tn(score_grad, query_ref[:, lanes])
        value_acc[lanes, :] += mm_tn(prob, part)
    query_grad = jnp.concatenate(pieces, 1)
    normed2_grad = back(query_grad, normed2_ref[...], w_query_ref, 1)
    resid1_grad = resid2_grad + norm_back(resid1_ref[...], gain_ref[1:2, :], normed2_grad)
    resid1_grad_ref[...] = resid1_grad
    attended_grad_ref[...] = back(resid1_grad.astype(BF), attended_ref[...], w_self_ref, 0).astype(BF)

    @pl.when(at == pl.num_programs(0) - 1)
    def _():
        col = lax.broadcasted_iota(jnp.int32, (keys, wide), 1) // HEAD
        for group in range(model // wide):
            lanes = slice(group * wide, (group + 1) * wide)
            key_sum = jnp.zeros((keys, wide), F32)
            value_sum = jnp.zeros((keys, wide), F32)
            for head in range(4):
                rows = slice(group * wide + head * keys, group * wide + (head + 1) * keys)
                key_sum = jnp.where(col == head, key_acc[rows, :], key_sum)
                value_sum = jnp.where(col == head, value_acc[rows, :], value_sum)
            memory_ref[0, :, lanes] = (key_sum * SCALE).astype(BF)
            memory_ref[1, :, lanes] = value_sum.astype(BF)


def middle_back(gu, more, cotangent, kept, packed, starts, adapters, gains, keys, values):
    row_count, model = gu.shape
    step = min(row_count, 128)
    attended, resid1, normed2, query, probs, crossed, resid2, latents = kept
    (w_self, spec_self), (w_query, spec_query), (w_cross, spec_cross) = [square(packed, at) for at in starts]
    rows = pl.BlockSpec((step, model), lambda at: (at, 0))
    scratch = pltpu.VMEM((model // HEAD * keys.shape[0], 4 * HEAD), BF)
    wider = pltpu.VMEM((model // HEAD * keys.shape[0], 4 * HEAD), F32)
    memory = (2,) + keys.shape
    return pl.pallas_call(
        middle_back_kernel,
        grid=(row_count // step,),
        in_specs=[rows] * 10
        + [pl.BlockSpec((step, 48), lambda at: (at, 0)), spec_self, spec_query, spec_cross]
        + [once(item.shape) for item in (adapters, gains, keys, values)],
        out_specs=[rows, rows, whole(memory), whole(adapters.shape)],
        out_shape=[
            jax.ShapeDtypeStruct((row_count, model), F32),
            jax.ShapeDtypeStruct((row_count, model), BF),
            jax.ShapeDtypeStruct(memory, BF),
            jax.ShapeDtypeStruct(adapters.shape, F32),
        ],
        scratch_shapes=[scratch, scratch, wider, wider],
        compiler_params=params(),
        cost_estimate=cost(6 * row_count * model * model, 6 * model * model + 36 * row_count * model),
        name="middle_back",
    )(
        gu, more, cotangent, resid2, resid1, normed2, query, probs, crossed, attended, latents,
        w_self, w_query, w_cross, adapters, gains, keys, values,
    )


def qkv_back_kernel(
    place_ref, grad_ref, normed_ref, lat_ref, down_ref, up_ref, w_ref, gu_ref, gdown_ref, gup_ref, gu_acc, glat_acc
):
    at = pl.program_id(0)
    gradient = grad_ref[...]
    direct = mm_nt(gradient, w_ref[...])
    glat = mm_nt(gradient, up_ref[...])
    gup_ref[...] = mm_tn(lat_ref[...], gradient)

    @pl.when(at == 0)
    def _():
        gu_acc[...] = direct
        glat_acc[...] = glat

    @pl.when(at > 0)
    def _():
        gu_acc[...] += direct
        glat_acc[...] += glat

    @pl.when(at == pl.num_programs(0) - 1)
    def _():
        low = glat_acc[...].astype(BF)
        gu_ref[...] = (gu_acc[...] + mm(low, down_ref[...])).astype(gu_ref.dtype)
        gdown_ref[...] = mm_tn(low, normed_ref[...])


def qkv_back(place, row_count, gradient, normed, latent, down, up, packed, start, kind):
    model = normed.shape[1]
    width = gradient.shape[2]
    ranks = down.shape[0]
    if start % width == 0 and width % LANES == 0:
        weight, spec = packed, pl.BlockSpec((model, width), lambda at, ref: (0, start // width + at))
    else:
        weight = packed[:, start : start + 3 * width].reshape(model, 3, width).transpose(1, 0, 2)
        spec = pl.BlockSpec((None, model, width), lambda at, ref: (at, 0, 0))
    part = pl.BlockSpec((None, ranks, width), lambda at, ref: (at, 0, 0))
    return pl.pallas_call(
        qkv_back_kernel,
        grid_spec=pltpu.PrefetchScalarGridSpec(
            num_scalar_prefetch=1,
            grid=(3,),
            in_specs=[
                pl.BlockSpec((None, row_count, width), lambda at, ref: (at, ref[0], 0)),
                pl.BlockSpec((row_count, model), lambda at, ref: (ref[0], 0)),
                pl.BlockSpec((row_count, ranks), lambda at, ref: (ref[0], 0)),
                whole(down.shape),
                part,
                spec,
            ],
            out_specs=[whole((row_count, model)), whole((ranks, model)), part],
            scratch_shapes=[pltpu.VMEM((row_count, model), F32), pltpu.VMEM((row_count, ranks), F32)],
        ),
        out_shape=[
            jax.ShapeDtypeStruct((row_count, model), kind),
            jax.ShapeDtypeStruct((ranks, model), F32),
            jax.ShapeDtypeStruct((3, ranks, width), F32),
        ],
        compiler_params=params(),
        cost_estimate=cost(6 * row_count * model * width, 6 * model * width + 8 * row_count * model),
        name="qkv_back",
    )(place, gradient, normed, latent, down, up, weight)


def body(
    inputs,
    text_states,
    adapter_index,
    norm_gains,
    norm_biases,
    self_in,
    self_out,
    cross_query,
    cross_text,
    cross_out,
    hidden_in,
    hidden_out,
    adapter_down,
    adapter_up,
    cotangent,
    *,
    sizes,
):
    seq, fsdp = sizes
    spot = lax.axis_index("seq")
    local = self_in.shape[0]
    model = inputs.shape[2]
    rows = inputs.shape[1]
    frames = rows * seq
    wide = model // seq
    hidden_all = hidden_in.shape[1]
    hidden = hidden_all // seq
    adapters, rank, piece = adapter_down.shape
    total = piece * fsdp

    def swap(value):
        return lax.ppermute(value, "seq", [(0, 1), (1, 0)])

    def pick(value, axis, extent):
        return lax.dynamic_slice_in_dim(value, spot * extent, extent, axis)

    def joined(mine, other, axis):
        return jnp.where(
            spot == 0, jnp.concatenate([mine, other], axis), jnp.concatenate([other, mine], axis)
        )

    def gather(value, axis):
        if seq == 2:
            return joined(value, swap(value), axis)
        return lax.all_gather(value, "seq", axis=axis, tiled=True)

    def after(value, *others):
        return lax.optimization_barrier((value,) + others)[0]

    index_all = lax.all_to_all(jnp.broadcast_to(adapter_index, (fsdp,)), "fsdp", 0, 0, tiled=True)
    table = jnp.concatenate([adapter_down, adapter_up], 1)
    picked = jnp.take(table, index_all, axis=0)
    arrived = lax.all_to_all(picked, "fsdp", 0, 0, tiled=True)
    chosen = arrived.transpose(1, 0, 2).reshape(2 * rank, total)
    down_all, upper_all = chosen[:rank], chosen[rank:]
    in_cuts = [0, 3 * model, 4 * model, 5 * model, 7 * model, 8 * model, 9 * model, 9 * model + hidden_all]
    out_cuts = [0, 3 * model, 4 * model, 5 * model, 7 * model, 8 * model, 8 * model + hidden_all, 9 * model + hidden_all]
    downs = [down_all[:, in_cuts[at] : in_cuts[at + 1]] for at in range(7)]
    uppers = [upper_all[:, out_cuts[at] : out_cuts[at + 1]] for at in range(7)]

    def own_parts(matrix, parts):
        return lax.dynamic_index_in_dim(matrix.reshape(-1, parts, seq, wide), spot, 2, False)

    def part_down(matrix, parts):
        return matrix.reshape(rank, parts, model).transpose(1, 0, 2).reshape(parts * rank, model)

    def part_upper(matrix, parts):
        own = own_parts(matrix, parts).transpose(1, 0, 2)
        eye = jnp.eye(parts, dtype=BF)[:, :, None, None]
        return (eye * own[:, None]).reshape(parts, parts * rank, wide)

    own_in = own_parts(self_in, 3).reshape(local, 3 * wide)
    own_text = own_parts(cross_text, 2).reshape(local, 2 * wide)
    first = jnp.concatenate([self_out, cross_query, cross_out, own_in, own_text], 1)
    starts = (0, model, 2 * model)
    start_in, start_text = 3 * model, 3 * model + 3 * wide
    packed = lax.all_gather(first, "fsdp", axis=0, tiled=True)
    depth = hidden_out.shape[0] // seq
    merged = depth % local == 0
    if merged:
        folds = depth // local
        unit_shape = (fsdp, seq, folds, local)

        def own_units(matrix):
            kept = lax.dynamic_index_in_dim(matrix.reshape((-1,) + unit_shape), spot, 2, False)
            return kept.transpose(0, 2, 1, 3).reshape(-1, hidden)

        def place_units(matrix):
            kept = matrix.reshape(-1, folds, fsdp, local).transpose(0, 2, 1, 3)[:, :, None]
            return put(kept, 2).reshape(-1, hidden_all)

        low = pick(hidden_out, 0, depth).reshape(folds, local, model).transpose(1, 0, 2)
        second = jnp.concatenate([own_units(hidden_in), low.reshape(local, folds * model)], 1)
        packed_feed = lax.all_gather(second, "fsdp", axis=0, tiled=True)

        def feed_weights(block):
            per = model // block
            return (
                packed_feed,
                pl.BlockSpec((model, block), lambda at: (0, at)),
                packed_feed,
                pl.BlockSpec((block, model), lambda at: (at % per, folds + at // per)),
            )
    else:

        def own_units(matrix):
            kept = lax.dynamic_index_in_dim(matrix.reshape(-1, fsdp, seq, depth), spot, 2, False)
            return kept.reshape(-1, hidden)

        def place_units(matrix):
            return put(matrix.reshape(-1, fsdp, 1, depth), 2).reshape(-1, hidden_all)

        whole_in = lax.all_gather(own_units(hidden_in), "fsdp", axis=0, tiled=True)
        whole_out = lax.all_gather(pick(hidden_out, 0, depth), "fsdp", axis=0, tiled=True)

        def feed_weights(block):
            return (
                whole_in,
                pl.BlockSpec((model, block), lambda at: (0, at)),
                whole_out,
                pl.BlockSpec((block, model), lambda at: (at, 0)),
            )

    def put(value, axis):
        shape = list(value.shape)
        shape[axis] = seq
        return lax.dynamic_update_slice_in_dim(jnp.zeros(shape, value.dtype), value, spot, axis)

    frames_in = inputs[0]
    cot = cotangent[0]
    down_qkv, upper_qkv = part_down(downs[0], 3), part_upper(uppers[0], 3)
    x_all = gather(frames_in, 0)
    normed1, lat_qkv, triple = qkv_project(
        x_all, norm_gains[0:1], norm_biases[0:1], down_qkv, upper_qkv, packed, start_in, 3 * wide
    )
    padded = -(-wide // LANES) * LANES
    if padded != wide:
        triple = jnp.pad(triple.reshape(frames, 3, wide), ((0, 0), (0, 0), (0, padded - wide)))
        triple = triple.reshape(frames, 3 * padded)
    head_out, probs = attend(triple, padded)
    if seq == 2:
        mine = pick(head_out, 0, rows)
        theirs = lax.dynamic_slice_in_dim(head_out, (1 - spot) * rows, rows, 0)
        attended = joined(mine, swap(theirs), 1)
    else:
        attended = lax.all_to_all(head_out[:, :wide], "seq", split_axis=0, concat_axis=1, tiled=True)

    text = text_states[0]
    down_text, upper_text = part_down(downs[3], 2), part_upper(uppers[3], 2)
    w_text = packed[:, start_text : start_text + 2 * wide]
    flat_text = upper_text.transpose(1, 0, 2).reshape(2 * rank, 2 * wide)
    lat_text = mm_nt(text, down_text).astype(BF)
    memory = (mm(text, w_text) + mm(lat_text, flat_text)).astype(BF).reshape(-1, 2, wide)
    memory_all = gather(memory, 2)
    keys, values = memory_all[:, 0], memory_all[:, 1]

    square_adapters = jnp.concatenate([downs[1], uppers[1], downs[2], uppers[2], downs[4], uppers[4]], 0)
    resid1, normed2, query, cross_probs, crossed, resid2, normed3, latents = middle(
        attended, frames_in, packed, starts, square_adapters, norm_gains, norm_biases, keys, values
    )

    feed_adapters = (downs[5], own_units(uppers[5]), own_units(downs[6]), uppers[6])
    if seq == 2:
        cot_other = swap(after(cot, x_all))
        normed3_other = swap(normed3)
        theirs = feed_forward(normed3_other, cot_other, *feed_adapters, feed_weights, hidden, BF)
        ours = feed_forward(after(normed3, theirs[1]), cot, *feed_adapters, feed_weights, hidden, F32)
        gu_more = swap(theirs[1])
        out_more = swap(after(theirs[0], gu_more))
        output = (resid2 + ours[0] + out_more.astype(F32)).astype(BF)
        gu = ours[1]
        feed_grads = [one + two for one, two in zip(ours[2:], theirs[2:])]
    else:
        all_out = feed_forward(gather(normed3, 0), gather(cot, 0), *feed_adapters, feed_weights, hidden, F32)
        summed = [
            lax.psum_scatter(item.astype(BF), "seq", scatter_dimension=0, tiled=True) for item in all_out[:2]
        ]
        output = (resid2 + summed[0].astype(F32)).astype(BF)
        gu, gu_more = summed[1], jnp.zeros_like(summed[1])
        feed_grads = all_out[2:]
    gdown_in, gup_in, gdown_out, gup_out = feed_grads

    kept = (attended, resid1, normed2, query, cross_probs, crossed, resid2, latents)
    resid1_grad, attended_grad, memory_part, square_grads = middle_back(
        gu, gu_more, cot, kept, packed, starts, square_adapters, norm_gains, keys, values
    )

    if seq == 2:
        other_part = lax.dynamic_slice_in_dim(memory_part, (1 - spot) * wide, wide, 2)
        memory_grad = (
            pick(memory_part, 2, wide).astype(F32) + swap(other_part).astype(F32)
        ).astype(BF)
    else:
        memory_grad = lax.psum_scatter(memory_part, "seq", scatter_dimension=2, tiled=True)
    memory_flat = memory_grad.transpose(1, 0, 2).reshape(-1, 2 * wide)
    glat_text = mm_nt(memory_flat, flat_text).astype(BF)
    gup_text = mm_tn(lat_text, memory_flat)
    gdown_text = mm_tn(glat_text, text)
    text_grad = mm_nt(memory_flat, w_text) + mm(glat_text, down_text)

    if seq == 2:
        grad_theirs = lax.dynamic_slice_in_dim(attended_grad, (1 - spot) * wide, wide, 1)
        head_grad = joined(pick(attended_grad, 1, wide), swap(grad_theirs), 0)
    else:
        head_grad = lax.all_to_all(attended_grad, "seq", split_axis=1, concat_axis=0, tiled=True)
        head_grad = jnp.pad(head_grad, ((0, 0), (0, padded - wide)))
    triple_grad = attend_back(triple, head_out, head_grad, probs, padded)[:, :, :wide]
    back = partial(
        qkv_back, gradient=triple_grad, normed=normed1, latent=lat_qkv, down=down_qkv, up=upper_qkv, packed=packed,
        start=start_in,
    )
    if seq == 2:
        there = back((1 - spot)[None], rows, kind=BF)
        here = back(after(spot, there[0])[None], rows, kind=F32)
        normed1_grad = here[0] + swap(there[0]).astype(F32)
        gdown_qkv, gup_qkv = there[1] + here[1], there[2] + here[2]
    else:
        full, gdown_qkv, gup_qkv = back(jnp.zeros((1,), jnp.int32), frames, kind=BF)
        normed1_grad = lax.psum_scatter(full, "seq", scatter_dimension=0, tiled=True).astype(F32)
    input_grad = resid1_grad + norm_back(frames_in.astype(F32), norm_gains[0:1], normed1_grad)

    def flat_down(grads, parts):
        return grads.reshape(parts, rank, model).transpose(1, 0, 2).reshape(rank, parts * model)

    def flat_upper(grads, parts):
        own = jnp.stack([grads[at, at * rank : (at + 1) * rank] for at in range(parts)], 1)
        return put(own[:, :, None], 2).reshape(rank, parts * model)

    gup_text = gup_text.reshape(2 * rank, 2, wide).transpose(1, 0, 2)
    squares = [square_grads[rank * at : rank * (at + 1)] for at in range(6)]
    down_grads = jnp.concatenate(
        [flat_down(gdown_qkv, 3), squares[0], squares[2], flat_down(gdown_text, 2), squares[4], gdown_in,
         place_units(gdown_out)], 1
    )
    upper_grads = jnp.concatenate(
        [flat_upper(gup_qkv, 3), squares[1], squares[3], flat_upper(gup_text, 2), squares[5], place_units(gup_in),
         gup_out], 1
    )
    sent = jnp.concatenate([down_grads, upper_grads], 0).astype(BF)
    sent = sent.reshape(2 * rank, fsdp, piece).transpose(1, 0, 2)
    received = lax.all_to_all(sent, "fsdp", 0, 0, tiled=True)
    selector = (index_all[None, :] == jnp.arange(adapters, dtype=jnp.int32)[:, None]).astype(BF)
    shares = jnp.einsum("ac,crw->arw", selector, received, preferred_element_type=F32)
    if seq == 2:
        shares = shares + swap(shares.astype(BF)).astype(F32)
        text_total = text_grad + swap(text_grad.astype(BF)).astype(F32)
    else:
        shares = lax.psum(shares.astype(BF), "seq").astype(F32)
        text_total = lax.psum(text_grad.astype(BF), "seq").astype(F32)
    return (output[None], input_grad[None], text_total[None], shares[:, :rank], shares[:, rank:])


def solution(mesh):
    return jax.shard_map(
        partial(body, sizes=(mesh.shape["seq"], mesh.shape["fsdp"])),
        mesh=mesh,
        in_specs=(
            P("fsdp", "seq", None),
            P("fsdp", None, None),
            P("fsdp"),
            P(),
            P(),
            P("fsdp", None),
            P("fsdp", None),
            P("fsdp", None),
            P("fsdp", None),
            P("fsdp", None),
            P("fsdp", None),
            P("fsdp", None),
            P(None, None, "fsdp"),
            P(None, None, "fsdp"),
            P("fsdp", "seq", None),
        ),
        out_specs=(
            P("fsdp", "seq", None),
            P("fsdp", "seq", None),
            P("fsdp", None, None),
            P(None, None, "fsdp"),
            P(None, None, "fsdp"),
        ),
        check_vma=False,
    )
```

time: 1670 us -> 600 us (0.36)
  local copies, waits for them, and re-layouts: 473 us -> 63.2 us
  waiting for transfers between devices: 585 us -> 200 us
  matrix products: 369 us -> 12.4 us
  Pallas kernels: 0 us -> 230 us
  other arithmetic: 177 us -> 31.5 us
    all_gather x9 -> x2, waiting for transfers between devices: 504 us -> 69.7 us  [the longest x1 69.7 us: body(): packed = lax.all_gather(first, 'fsdp', axis=0, tiled=True)]
    dot_general x74 -> x9, matrix products: 364 us -> 12.4 us  [the longest x3 4.94 us: mm_nt(): lax.dot_general(a, b, (((1,), (1,)), ((), ())), preferred_element_type=F32)]
    unnamed x318 -> x89, local copies, waits for them, and re-layouts: 260 us -> 10.3 us
    pallas_call x0 -> x9, Pallas kernels: none -> 230 us  [the longest x2 64.8 us: feed_forward(): pl.pallas_call(feed_kernel, grid=(hidden // block,), in_specs=[main, main...]
    ppermute x0 -> x12, waiting for transfers between devices: none -> 107 us  [swap(): return lax.ppermute(value, 'seq', [(0, 1), (1, 0)])]
    unnamed x13 -> x2, other arithmetic: 101 us -> 0.73 us
    all_gather x2 -> x0, local copies, waits for them, and re-layouts: 78 us -> none  [the longest x1 39.2 us: body(): lax.all_gather(adapter_down, 'fsdp', axis=2, tiled=True)]
    convert_element_type x8 -> x2, other arithmetic: 39.4 us -> 0.01 us  [part_upper(): eye = jnp.eye(parts, dtype=BF)[:, :, None, None]]
  transfers between devices with their start and end apart: 20 -> 17, of which waited for: 9 -> 10; matrix products, arithmetic and copies ran while one was open for 41% -> 15% of each run, Pallas kernels for 0% -> 26%
where the time goes in v1:
time: 600 us; the launch traced here: 591 us
  Pallas kernels  230 us (38%)
  waiting for transfers between devices  200 us (33%)
  local copies, waits for them, and re-layouts  63.2 us (11%)
  starting transfers between devices  37.5 us (6%)
  other arithmetic  31.5 us (5%)
  between operations  16 us (3%)
  matrix products  12.4 us (2%)
    ppermute x12, waiting for transfers between devices, swap(): return lax.ppermute(value, 'seq', [(0, 1), (1, 0)])  107 us
    all_gather x1, waiting for transfers between devices, body(): packed = lax.all_gather(first, 'fsdp', axis=0, tiled=True)  69.7 us
    pallas_call x2, Pallas kernels, feed_forward(): pl.pallas_call(feed_kernel, grid=(hidden // block,), in_specs=[main, main...  64.8 us
    pallas_call x1, Pallas kernels, middle_back(): pl.pallas_call(middle_back_kernel, grid=(row_count // step,), in_specs=[r...  45.2 us
    pallas_call x1, Pallas kernels, middle(): pl.pallas_call(middle_kernel, grid=(row_count // step,), in_specs=[rows,...  31.3 us
    pallas_call x1, Pallas kernels, attend(): pl.pallas_call(attend_kernel, grid=(pairs,), in_specs=pair_specs(frames,...  28.3 us
    pallas_call x2, Pallas kernels, qkv_back(): pl.pallas_call(qkv_back_kernel, grid_spec=pltpu.PrefetchScalarGridSpec(nu...  22 us
    pallas_call x1, Pallas kernels, attend_back(): pl.pallas_call(attend_back_kernel, grid=(pairs,), in_specs=pair_specs(fra...  21.6 us
  transfers between devices with their start and end apart: 17, of which 10 were waited for; matrix products, arithmetic and copies ran while one was open for 15% of the time, Pallas kernels for 26%

profile of v1, /device:TPU:0, one launch (start us, length us, event | category | flops | bytes accessed | tf_op | source)
XLA Modules:
  0.0 591.0 jit_solution(9728395038679985030)
XLA Ops:
  19.8 5.5 reshape.219
  29.7 7.4 %all-to-all-start = ((s32[16,1,1]{2,1,0:T(1,128)}), s32[16,1,1]{2,1,0:T(1,128)S(1)}, u32[]{:S(2)}, u32[]{:S(2)}) async-start(s32[16,1,1]{2,1,0:T(1,128)} %broadcast_in_dim.61), calls=%async_computation | async-start | bytes 16384 | tf_op jit(solution)/shard_map/all_to_all | solution.py:613
  37.2 6.4 %all-to-all-done = s32[16,1,1]{2,1,0:T(1,128)S(1)} async-done(((s32[16,1,1]{2,1,0:T(1,128)}), s32[16,1,1]{2,1,0:T(1,128)S(1)}, u32[]{:S(2)}, u32[]{:S(2)}) %all-to-all-start) | async-done | bytes 96 | tf_op jit(solution)/shard_map/all_to_all | solution.py:613
  45.8 4.7 all-to-all-start.1
  55.7 31.7 %collective-permute-done = bf16[512,1536]{1,0:T(8,128)(2,1)} collective-permute-done((bf16[512,1536]{1,0:T(8,128)(2,1)S(1)}, bf16[512,1536]{1,0:T(8,128)(2,1)}, u32[]{:S(2)}, u32[]{:S(2)}) %collective-permute-start) | collective-permute-done | bytes 1572896 | tf_op jit(solution)/shard_map/ppermute | solution.py:595
  92.5 6.4 %all-to-all-done.1 = bf16[16,32,1248]{2,1,0:T(8,128)(2,1)} async-done(((bf16[16,32,1248]{2,1,0:T(8,128)(2,1)}), bf16[16,32,1248]{2,1,0:T(8,128)(2,1)}, u32[]{:S(2)}, u32[]{:S(2)}) %all-to-all-start.1) | async-done | bytes 1277984 | tf_op jit(solution)/shard_map/all_to_all | solution.py:616
  105.8 69.7 %all-gather.3.cloned.1.call-done.w_ref.w_self_ref.w_query_ref.w_cross_ref = bf16[1536,8448]{1,0:T(8,128)(2,1)} async-done(((bf16[96,8448]{1,0:T(8,128)(2,1)}), bf16[1536,8448]{1,0:T(8,128)(2,1)}) %all-gather.3.cloned.1.call-update) | async-done | bytes 25952272 | tf_op jit(solution)/shard_map/all_gather | solution.py:640
  175.6 17.0 %qkv_project.1 = (bf16[1024,1536]{1,0:T(8,128)(2,1)}, bf16[1024,48]{1,0:T(8,128)(2,1)}, bf16[1024,2304]{1,0:T(8,128)(2,1)}) custom-call(bf16[1024,1536]{1,0:T(8,128)(2,1)} %maximum_select_fusion.x_ref, f32[1,1536]{1,0:T(1,128)} %get-tuple-element.131.gain_ref, f32[1,1536]{1,0:T(1,128)} %slice.116.bias_ref, bf16[48,1536]{1,0:T(8,128)(2,1)} %bitcast.174, ...), custom_call_target="tpu_custom_call" | custom-call | flops 7247757312 | bytes 10223616 | tf_op jit(solution)/shard_map/qkv_project/pallas_call | solution.py:112
  192.6 28.3 %attend.1 = (bf16[1024,768]{1,0:T(8,128)(2,1)}, bf16[12,2560,256]{2,1,0:T(8,128)(2,1)}) custom-call(bf16[1024,2304]{1,0:T(8,128)(2,1)} %get-tuple-element.44.q_ref.k_ref.v_ref, bf16[1024,2304]{1,0:T(8,128)(2,1)} %get-tuple-element.44.q_ref.k_ref.v_ref, bf16[1024,2304]{1,0:T(8,128)(2,1)} %get-tuple-element.44.q_ref.k_ref.v_ref), custom_call_target="tpu_custom_call" | custom-call | flops 2013265920 | bytes 22020096 | tf_op jit(solution)/shard_map/attend/pallas_call | solution.py:166
  229.6 16.7 %collective-permute-done.2 = bf16[64,2,768]{2,0,1:T(8,128)(2,1)S(1)} collective-permute-done((bf16[64,2,768]{2,0,1:T(8,128)(2,1)S(1)}, bf16[64,2,768]{2,0,1:T(8,128)(2,1)S(1)}, u32[]{:S(2)}, u32[]{:S(2)}) %collective-permute-start.2) | collective-permute-done | bytes 196640 | tf_op jit(solution)/shard_map/ppermute | solution.py:595
  248.8 31.3 %middle.1 = (f32[512,1536]{1,0:T(8,128)}, bf16[512,1536]{1,0:T(8,128)(2,1)}, bf16[512,1536]{1,0:T(8,128)(2,1)}, bf16[512,1536]{1,0:T(8,128)(2,1)}, bf16[512,1536...) custom-call(bf16[512,1536]{1,0:T(8,128)(2,1)} %maximum_select_fusion.1.attended_ref, ...), custom_call_target="tpu_custom_call" | custom-call | flops 7247757312 | bytes 33030144 | tf_op jit(solution)/shard_map/middle/pallas_call | solution.py:391
  284.9 31.2 %collective-permute-done.3.normed_ref = bf16[512,1536]{1,0:T(8,128)(2,1)} collective-permute-done((bf16[512,1536]{1,0:T(8,128)(2,1)}, bf16[512,1536]{1,0:T(8,128)(2,1)}, u32[]{:S(2)}, u32[]{:S(2)}) %collective-permute-start.3) | collective-permute-done | bytes 1572896 | tf_op jit(solution)/shard_map/ppermute | solution.py:595
  316.1 32.1 %feed_forward.2 = (bf16[512,1536]{1,0:T(8,128)(2,1)}, bf16[512,1536]{1,0:T(8,128)(2,1)}, f32[16,1536]{1,0:T(8,128)}, f32[16,3072]{1,0:T(8,128)}, f32[16,3072]{1,0:T(8,128)}, /*index=5*/f32[16,1536]{1,0:T(8,128)}) custom-call(bf16[512,1536]{1,0:T(8,128)(2,1)} %collective-permute-done.3.normed_ref, bf16[512,1536]{1,0:T(8,128)(2,1)} %collective-permute-done.4.cot_ref, ...), custom_call_target="tpu_custom_call" | custom-call | flops 19327352832 | bytes 18874368 | tf_op jit(solution)/shard_map/feed_forward/pallas_call | solution.py:294
  349.8 32.7 %feed_forward.3 = (f32[512,1536]{1,0:T(8,128)}, f32[512,1536]{1,0:T(8,128)}, f32[16,1536]{1,0:T(8,128)}, f32[16,3072]{1,0:T(8,128)}, f32[16,3072]{1,0:T(8,128)}, /*index=5*/f32[16,1536]{1,0:T(8,128)}) custom-call(bf16[512,1536]{1,0:T(8,128)(2,1)} %get-tuple-element.50.normed_ref, bf16[512,1536]{1,0:T(8,128)(2,1)} %bitcast.20.cot_ref, ...), custom_call_target="tpu_custom_call" | custom-call | flops 19327352832 | bytes 18874368 | tf_op jit(solution)/shard_map/feed_forward/pallas_call | solution.py:294
  385.2 45.2 %middle_back.1 = (f32[512,1536]{1,0:T(8,128)}, bf16[512,1536]{1,0:T(8,128)(2,1)}, bf16[2,64,1536]{2,1,0:T(8,128)(2,1)}, f32[96,1536]{1,0:T(8,128)}) custom-call(f32[512,1536]{1,0:T(8,128)} %get-tuple-element.54.gu_ref, bf16[512,1536]{1,0:T(8,128)(2,1)} %collective-permute-done.5.more_ref, bf16[512,1536]{1,0:T(8,128)(2,1)} %bitcast.20.cot_ref, ...), custom_call_target="tpu_custom_call" | custom-call | flops 7247757312 | bytes 42467328 | tf_op jit(solution)/shard_map/middle_back/pallas_call | solution.py:477
  450.7 7.5 %collective-permute-done.7 = bf16[512,768]{1,0:T(8,128)(2,1)} collective-permute-done((bf16[512,768]{1,0:T(8,128)(2,1)}, bf16[512,768]{1,0:T(8,128)(2,1)}, u32[]{:S(2)}, u32[]{:S(2)}) %collective-permute-start.7) | collective-permute-done | bytes 786464 | tf_op jit(solution)/shard_map/ppermute | solution.py:595
  461.3 21.6 %attend_back.1.grad_ref = bf16[3,1024,768]{2,1,0:T(8,128)(2,1)} custom-call(bf16[1024,2304]{1,0:T(8,128)(2,1)} %get-tuple-element.44.q_ref.k_ref.v_ref, bf16[1024,2304]{1,0:T(8,128)(2,1)} %get-tuple-element.44.q_ref.k_ref.v_ref, bf16[1024,2304]{1,0:T(8,128)(2,1)} %get-tuple-element.44.q_ref.k_ref.v_ref, bf16[1024,768]{1,0:T(8,128)(2,1)} %get-tuple-element.45.out_ref, ...), custom_call_target="tpu_custom_call" | custom-call | flops 4026531840 | bytes 28311552 | tf_op jit(solution)/shard_map/attend_back/pallas_call | solution.py:223
  482.9 10.7 %qkv_back.2 = (bf16[512,1536]{1,0:T(8,128)(2,1)}, f32[48,1536]{1,0:T(8,128)}, f32[3,48,768]{2,1,0:T(8,128)}) custom-call(s32[1]{0:T(128)} %bitcast.30.place_ref, bf16[3,1024,768]{2,1,0:T(8,128)(2,1)} %attend_back.1.grad_ref, bf16[1024,1536]{1,0:T(8,128)(2,1)} %get-tuple-element.64.normed_ref, bf16[1024,48]{1,0:T(8,128)(2,1)} %get-tuple-element.65.lat_ref, ...), custom_call_target="tpu_custom_call" | custom-call | flops 3623878656 | bytes 13369344 | tf_op jit(solution)/shard_map/qkv_back/pallas_call | solution.py:536
  495.1 11.3 %qkv_back.3 = (f32[512,1536]{1,0:T(8,128)}, f32[48,1536]{1,0:T(8,128)}, f32[3,48,768]{2,1,0:T(8,128)}) custom-call(s32[1]{0:T(128)} %bitcast.31.place_ref, bf16[3,1024,768]{2,1,0:T(8,128)(2,1)} %attend_back.1.grad_ref, bf16[1024,1536]{1,0:T(8,128)(2,1)} %get-tuple-element.64.normed_ref, bf16[1024,48]{1,0:T(8,128)(2,1)} %get-tuple-element.65.lat_ref, ...), custom_call_target="tpu_custom_call" | custom-call | flops 3623878656 | bytes 13369344 | tf_op jit(solution)/shard_map/qkv_back/pallas_call | solution.py:536
  523.1 11.3 %all-to-all-start.2 = ((bf16[16,32,1248]{2,1,0:T(8,128)(2,1)}), bf16[16,32,1248]{2,1,0:T(8,128)(2,1)}, u32[]{:S(2)}, u32[]{:S(2)}) async-start(bf16[16,32,1248]{2,1,0:T(8,128)(2,1)} %copy.111), calls=%async_computation.2 | async-start | bytes 2621440 | tf_op jit(solution)/shard_map/all_to_all | solution.py:804
  535.3 6.8 %collective-permute-done.10 = bf16[64,1536]{1,0:T(8,128)(2,1)S(1)} collective-permute-done((bf16[64,1536]{1,0:T(8,128)(2,1)S(1)}, bf16[64,1536]{1,0:T(8,128)(2,1)S(1)}, u32[]{:S(2)}, u32[]{:S(2)}) %collective-permute-start.10) | collective-permute-done | bytes 196640 | tf_op jit(solution)/shard_map/ppermute | solution.py:595
  542.8 5.4 fusion.19
  550.8 11.0 %all-to-all-done.2 = bf16[16,32,1248]{2,1,0:T(8,128)(2,1)} async-done(((bf16[16,32,1248]{2,1,0:T(8,128)(2,1)}), bf16[16,32,1248]{2,1,0:T(8,128)(2,1)}, u32[]{:S(2)}, u32[]{:S(2)}) %all-to-all-start.2) | async-done | bytes 1277984 | tf_op jit(solution)/shard_map/all_to_all | solution.py:804
  569.0 12.7 %collective-permute-done.11 = bf16[8,32,1248]{2,0,1:T(8,128)(2,1)S(1)} collective-permute-done((bf16[8,32,1248]{2,0,1:T(8,128)(2,1)S(1)}, bf16[8,32,1248]{2,0,1:T(8,128)(2,1)S(1)}, u32[]{:S(2)}, u32[]{:S(2)}) %collective-permute-start.11) | collective-permute-done | bytes 639008 | tf_op jit(solution)/shard_map/ppermute | solution.py:595
  (231 shorter events, 110.5 us)
Async XLA Ops:
  7.2 20.0 %copy-start = (bf16[384,1536]{1,0:T(8,128)(2,1)S(1)}, bf16[384,1536]{1,0:T(8,128)(2,1)}, u32[]{:S(2)}) copy-start(bf16[384,1536]{1,0:T(8,128)(2,1)} %param.26) | copy-start | bytes 3538948
  7.2 168.4 %all-gather.3.cloned.1.call-start = ((), (), s32[]{:S(2)}) async-start(), calls=%async_computation.3 | async-start | bytes 27574272 | tf_op jit(solution)/shard_map/all_gather | solution.py:640
  19.2 265.7 %all-gather.5.cloned.1.call-start = ((), (), s32[]{:S(2)}) async-start(), calls=%async_computation.4 | async-start | bytes 20054016 | tf_op jit(solution)/shard_map/all_gather | solution.py:657
  29.7 13.8 %all-to-all-start = ((s32[16,1,1]{2,1,0:T(1,128)}), s32[16,1,1]{2,1,0:T(1,128)S(1)}, u32[]{:S(2)}, u32[]{:S(2)}) async-start(s32[16,1,1]{2,1,0:T(1,128)} %broadcast_in_dim.61), calls=%async_computation | async-start | bytes 16384 | tf_op jit(solution)/shard_map/all_to_all | solution.py:613
  45.8 53.0 %all-to-all-start.1 = ((bf16[16,32,1248]{2,1,0:T(8,128)(2,1)}), bf16[16,32,1248]{2,1,0:T(8,128)(2,1)}, u32[]{:S(2)}, u32[]{:S(2)}) async-start(bf16[16,32,1248]{2,1,0:T(8,128)(2,1)} %broadcast_select_fusion), calls=%async_computation.1 | async-start | bytes 2621440 | tf_op jit(solution)/shard_map/all_to_all | solution.py:616
  50.6 36.9 %collective-permute-start = (bf16[512,1536]{1,0:T(8,128)(2,1)S(1)}, bf16[512,1536]{1,0:T(8,128)(2,1)}, u32[]{:S(2)}, u32[]{:S(2)}) collective-permute-start(bf16[512,1536]{1,0:T(8,128)(2,1)S(1)} %bitcast.171), channel_id=1, source_target_pairs={{0,16},{16,0},{1,17},{17,1},{2,18},{18,2},{3,19},{19,3},{4,20},{20... | collective-permute-start | bytes 4718600 | tf_op jit(solution)/shard_map/ppermute | solution.py:595
  91.0 193.9 %collective-permute-start.4 = (bf16[512,1536]{1,0:T(8,128)(2,1)}, bf16[512,1536]{1,0:T(8,128)(2,1)}, u32[]{:S(2)}, u32[]{:S(2)}) collective-permute-start(bf16[512,1536]{1,0:T(8,128)(2,1)} %bitcast.20.cot_ref), channel_id=1, source_target_pairs={{0,16},{16,0},{1,17},{17,1},{2,18},{18,2},{3,19},{19,3},{4,20},{20... | collective-permute-start | bytes 4718600 | tf_op jit(solution)/shard_map/ppermute | solution.py:595
  222.5 24.8 %collective-permute-start.1 = (bf16[512,768]{1,0:T(8,128)(2,1)S(1)}, bf16[512,768]{1,0:T(8,128)(2,1)S(1)}, u32[]{:S(2)}, u32[]{:S(2)}) collective-permute-start(bf16[512,768]{1,0:T(8,128)(2,1)S(1)} %get-tuple-element.108), channel_id=1, source_target_pairs={{0,16},{16,0},{1,17},{17,1},{2,18},{18,2},{3,19},{19,3},{4,20},{20... | collective-permute-start | bytes 2359304 | tf_op jit(solution)/shard_map/ppermute | solution.py:595
  227.7 18.6 %collective-permute-start.2 = (bf16[64,2,768]{2,0,1:T(8,128)(2,1)S(1)}, bf16[64,2,768]{2,0,1:T(8,128)(2,1)S(1)}, u32[]{:S(2)}, u32[]{:S(2)}) collective-permute-start(bf16[64,2,768]{2,0,1:T(8,128)(2,1)S(1)} %bitcast.187), channel_id=1, source_target_pairs={{0,16},{16,0},{1,17},{17,1},{2,18},{18,2},{3,19},{19,3},{4,20},{20... | collective-permute-start | bytes 589832 | tf_op jit(solution)/shard_map/ppermute | solution.py:595
  248.7 32.8 %copy-start.3 = (bf16[1,512,1536]{2,1,0:T(8,128)(2,1)S(1)}, bf16[1,512,1536]{2,1,0:T(8,128)(2,1)}, u32[]{:S(2)}) copy-start(bf16[1,512,1536]{2,1,0:T(8,128)(2,1)} %param.15) | copy-start | bytes 4718596
  280.0 36.1 %collective-permute-start.3 = (bf16[512,1536]{1,0:T(8,128)(2,1)}, bf16[512,1536]{1,0:T(8,128)(2,1)}, u32[]{:S(2)}, u32[]{:S(2)}) collective-permute-start(bf16[512,1536]{1,0:T(8,128)(2,1)} %get-tuple-element.50.normed_ref), channel_id=1, source_target_pairs={{0,16},{16,0},{1,17},{17,1},{2,18},{18,2},{3,19},{19,3},{4,20},{20... | collective-permute-start | bytes 4718600 | tf_op jit(solution)/shard_map/ppermute | solution.py:595
  348.2 34.3 %copy-start.23 = (f32[16,3072]{1,0:T(8,128)S(1)}, f32[16,3072]{1,0:T(8,128)}, u32[]{:S(2)}) copy-start(f32[16,3072]{1,0:T(8,128)} %get-tuple-element.76) | copy-start | bytes 589828
  348.2 35.4 %copy-start.22 = (f32[16,3072]{1,0:T(8,128)S(1)}, f32[16,3072]{1,0:T(8,128)}, u32[]{:S(2)}) copy-start(f32[16,3072]{1,0:T(8,128)} %get-tuple-element.80) | copy-start | bytes 589828
  348.2 36.9 %collective-permute-start.5 = (bf16[512,1536]{1,0:T(8,128)(2,1)}, bf16[512,1536]{1,0:T(8,128)(2,1)}, u32[]{:S(2)}, u32[]{:S(2)}) collective-permute-start(bf16[512,1536]{1,0:T(8,128)(2,1)} %get-tuple-element.49), channel_id=1, source_target_pairs={{0,16},{16,0},{1,17},{17,1},{2,18},{18,2},{3,19},{19,3},{4,20},{20... | collective-permute-start | bytes 4718600 | tf_op jit(solution)/shard_map/ppermute | solution.py:595
  432.0 7.5 %collective-permute-start.9 = (bf16[2,64,768]{2,1,0:T(8,128)(2,1)}, bf16[2,64,768]{2,1,0:T(8,128)(2,1)S(1)}, u32[]{:S(2)}, u32[]{:S(2)}) collective-permute-start(bf16[2,64,768]{2,1,0:T(8,128)(2,1)} %constant_dynamic-slice_fusion), channel_id=1, source_target_pairs={{0,16},{16,0},{1,17},{17,1},{2,18},{18,2},{3,19},{19,3},{4,20},{20... | collective-permute-start | bytes 589832 | tf_op jit(solution)/shard_map/ppermute | solution.py:595
  437.4 20.8 %collective-permute-start.7 = (bf16[512,768]{1,0:T(8,128)(2,1)}, bf16[512,768]{1,0:T(8,128)(2,1)}, u32[]{:S(2)}, u32[]{:S(2)}) collective-permute-start(bf16[512,768]{1,0:T(8,128)(2,1)} %get-tuple-element.106), channel_id=1, source_target_pairs={{0,16},{16,0},{1,17},{17,1},{2,18},{18,2},{3,19},{19,3},{4,20},{20... | collective-permute-start | bytes 2359304 | tf_op jit(solution)/shard_map/ppermute | solution.py:595
  438.9 103.9 %collective-permute-start.6 = (bf16[512,1536]{1,0:T(8,128)(2,1)}, bf16[512,1536]{1,0:T(8,128)(2,1)}, u32[]{:S(2)}, u32[]{:S(2)}) collective-permute-start(bf16[512,1536]{1,0:T(8,128)(2,1)} %get-tuple-element.53), channel_id=1, source_target_pairs={{0,16},{16,0},{1,17},{17,1},{2,18},{18,2},{3,19},{19,3},{4,20},{20... | collective-permute-start | bytes 4718600 | tf_op jit(solution)/shard_map/ppermute | solution.py:595
  493.6 54.6 %collective-permute-start.8 = (bf16[512,1536]{1,0:T(8,128)(2,1)}, bf16[512,1536]{1,0:T(8,128)(2,1)}, u32[]{:S(2)}, u32[]{:S(2)}) collective-permute-start(bf16[512,1536]{1,0:T(8,128)(2,1)} %get-tuple-element.66), channel_id=1, source_target_pairs={{0,16},{16,0},{1,17},{17,1},{2,18},{18,2},{3,19},{19,3},{4,20},{20... | collective-permute-start | bytes 4718600 | tf_op jit(solution)/shard_map/ppermute | solution.py:595
  495.1 11.3 %copy-start.15 = (f32[3,48,768]{2,1,0:T(8,128)S(1)}, f32[3,48,768]{2,1,0:T(8,128)}, u32[]{:S(2)}) copy-start(f32[3,48,768]{2,1,0:T(8,128)} %get-tuple-element.77) | copy-start | bytes 1327108
  523.1 11.3 %copy-start.16 = (f32[64,1536]{1,0:T(8,128)S(1)}, f32[64,1536]{1,0:T(8,128)}, u32[]{:S(2)}) copy-start(f32[64,1536]{1,0:T(8,128)} %fusion) | copy-start | bytes 1179652
  523.1 38.7 %all-to-all-start.2 = ((bf16[16,32,1248]{2,1,0:T(8,128)(2,1)}), bf16[16,32,1248]{2,1,0:T(8,128)(2,1)}, u32[]{:S(2)}, u32[]{:S(2)}) async-start(bf16[16,32,1248]{2,1,0:T(8,128)(2,1)} %copy.111), calls=%async_computation.2 | async-start | bytes 2621440 | tf_op jit(solution)/shard_map/all_to_all | solution.py:804
  534.7 7.4 %collective-permute-start.10 = (bf16[64,1536]{1,0:T(8,128)(2,1)S(1)}, bf16[64,1536]{1,0:T(8,128)(2,1)S(1)}, u32[]{:S(2)}, u32[]{:S(2)}) collective-permute-start(bf16[64,1536]{1,0:T(8,128)(2,1)S(1)} %get-tuple-element.132), channel_id=1, source_target_pairs={{0,16},{16,0},{1,17},{17,1},{2,18},{18,2},{3,19},{19,3},{4,20},{20... | collective-permute-start | bytes 589832 | tf_op jit(solution)/shard_map/ppermute | solution.py:595
  548.3 13.6 %copy-start.30 = (s32[16]{0:T(128)S(1)}, s32[16]{0:T(128)}, u32[]{:S(2)}) copy-start(s32[16]{0:T(128)} %copy-done.29) | copy-start | bytes 196
  564.2 17.5 %collective-permute-start.11 = (bf16[8,32,1248]{2,0,1:T(8,128)(2,1)S(1)}, bf16[8,32,1248]{2,0,1:T(8,128)(2,1)S(1)}, u32[]{:S(2)}, u32[]{:S(2)}) collective-permute-start(bf16[8,32,1248]{2,0,1:T(8,128)(2,1)S(1)} %get-tuple-element.134), channel_id=1, source_target_pairs={{0,16},{16,0},{1,17},{17,1},{2,18},{18,2},{3,19},{19,3},{4,20},{20... | collective-permute-start | bytes 1916936 | tf_op jit(solution)/shard_map/ppermute | solution.py:595
  (24 other events, 106.7 us)
Sparse Core Ops, SparseCore 0:
  19.3 156.1 all-gather.2
  177.2 105.1 all-gather.4
